TPU v7x, 256 devices: a whole 4x4x8 slice. The times are simulated.
256 devices in a mesh: ta: 4 (over z_lo, core), pa: 64 (over x, y, z_hi).
Axes of the slice: x: 4, y: 4, z: 8 (z_hi: 4, z_lo: 2; z = z_hi * 2 + z_lo), core: 2. Of those that a mesh axis runs over, the one named last changes fastest.
Arguments:
- green_freq: bfloat16 [256, 4, 256, 256], P('ta', None, 'pa'), may hold values from -6 to 6
- colloc: bfloat16 [4, 256, 1024], P(None, None, 'pa'), may hold values from -0.375 to 0.375
- core: bfloat16 [1024, 1024], replicated, may hold values from -0.1875 to 0.1875
Outputs:
- sigma_freq: bfloat16 [256, 4, 256, 256], P('ta', None, 'pa')
All inputs are finite; a program needn't handle non-finite values.
Results may differ from a plain program's by a relative error of at most 0.03.
Values may be sent and summed in bfloat16 or wider, within the bound.
No kernel may reach another device: no remote copies, remote signals or barrier semaphores. Data moves between devices by JAX's collectives and lax.ppermute only.
A program may use at most 128 MiB of HBM per device.

v0:
```python
import jax
import jax.numpy as jnp
from jax import lax
from jax.sharding import PartitionSpec as P

NFREQ = 128
NTIME = 128


def cut_along(array, dim, length):
    lengths = array.shape
    blocks = array.reshape(*lengths[:dim], length, lengths[dim] // length, *lengths[dim + 1 :])
    return jnp.moveaxis(blocks, dim, 0)


def summed_on_arrival(array, axis, dim):
    blocks = cut_along(array, dim, lax.axis_size(axis))
    arrived = lax.all_to_all(blocks, axis, split_axis=0, concat_axis=0, tiled=True)
    return arrived.astype(jnp.float32).sum(axis=0)


def time_tables(nfreq, ntime):
    freq = jnp.arange(nfreq, dtype=jnp.float32)
    times = jnp.arange(ntime, dtype=jnp.float32)
    phase = jnp.pi * (2.0 * freq[None, :] + 1.0) * (times[:, None] + 0.5) / ntime
    cosine = jnp.cos(phase)
    sine = jnp.sin(phase)
    scale_fwd = 1.0 / jnp.sqrt(jnp.float32(nfreq))
    scale_back = 1.0 / jnp.sqrt(jnp.float32(ntime))
    plus = jnp.concatenate([cosine, sine], axis=1) * scale_fwd
    minus = jnp.concatenate([-cosine, sine], axis=1) * scale_fwd
    fwd = jnp.stack([plus, minus], axis=0)
    back = jnp.concatenate([cosine.T, sine.T], axis=0) * scale_back
    return (fwd, back)


def local(green_freq, colloc, core):
    fwd, back = time_tables(NFREQ, NTIME)
    freq_rows = green_freq.shape[0]
    first = lax.axis_index("ta") * freq_rows
    fwd_part = lax.dynamic_slice_in_dim(fwd, first, freq_rows, 2)
    partial_time = jnp.einsum(
        "stw,wkij->stkij", fwd_part, green_freq.astype(jnp.float32), precision=lax.Precision.HIGHEST
    )
    green_time = summed_on_arrival(partial_time.astype(jnp.bfloat16), "ta", 1).astype(jnp.bfloat16)
    piece = lax.all_gather(colloc, "pa", axis=2, tiled=True)
    half_piece = jnp.einsum(
        "stkij,kjq->stkiq", green_time, piece, preferred_element_type=jnp.float32
    ).astype(jnp.bfloat16)
    gathered = piece[None, None]
    full_colloc = gathered[0, 0]
    kcount = full_colloc.shape[0]
    green_pts = jnp.einsum(
        "kip,stkiq->stkpq",
        full_colloc,
        lax.all_to_all(half_piece, "pa", split_axis=4, concat_axis=3, tiled=True),
        preferred_element_type=jnp.float32,
    )
    bubble_block = (jnp.sum(green_pts[0] * green_pts[1], axis=1) / kcount).astype(jnp.bfloat16)
    green_plus = green_pts[0]
    mixed = jnp.einsum(
        "pr,trq->tpq", core, bubble_block, preferred_element_type=jnp.float32
    ).astype(jnp.bfloat16)
    mixed_rows = lax.all_to_all(mixed, "pa", split_axis=1, concat_axis=2, tiled=True)
    screened_rows = jnp.einsum(
        "tps,sq->tpq", mixed_rows, core, preferred_element_type=jnp.float32
    ).astype(jnp.bfloat16)
    screened = lax.all_to_all(screened_rows, "pa", split_axis=2, concat_axis=1, tiled=True)
    source = (-green_plus * screened.astype(jnp.float32)[:, None]).astype(jnp.bfloat16)
    outer = jnp.einsum(
        "kip,tkpq->tkiq", full_colloc, source, preferred_element_type=jnp.float32
    ).astype(jnp.bfloat16)
    sigma_time = jnp.einsum(
        "tkiq,kjq->tkij",
        lax.all_to_all(outer, "pa", split_axis=2, concat_axis=3, tiled=True),
        full_colloc,
        preferred_element_type=jnp.float32,
    ).astype(jnp.bfloat16)
    time_rows = sigma_time.shape[0]
    first_time = lax.axis_index("ta") * time_rows
    back_part = lax.dynamic_slice_in_dim(back, first_time, time_rows, 1)
    partial_freq = jnp.einsum(
        "wt,tkij->wkij", back_part, sigma_time.astype(jnp.float32), precision=lax.Precision.HIGHEST
    )
    return summed_on_arrival(partial_freq.astype(jnp.bfloat16), "ta", 0).astype(jnp.bfloat16)


def solution(mesh):
    return jax.shard_map(
        local,
        mesh=mesh,
        in_specs=(P("ta", None, "pa", None), P(None, None, "pa"), P()),
        out_specs=P("ta", None, "pa", None),
        check_vma=False,
    )
```

profile of v0, /device:TPU:1, one launch (start us, length us, event | category | flops | bytes accessed | tf_op | source)
XLA Modules:
  0.0 482.2 jit_solution(289619318880138585)
XLA Ops:
  11.0 31.8 %all_to_all.73 = bf16[4,2,32,4,4,256]{5,2,4,3,1,0:T(8,128)(2,1)} all-to-all(bf16[4,2,32,4,4,256]{5,2,4,3,1,0:T(8,128)(2,1)S(1)} %bitcast.122), channel_id=1, replica_groups=mesh['ta'=4,'pa'=64] {'ta'}, dimensions={0} | all-to-all | bytes 4194304 | tf_op jit(solution)/shard_map/all_to_all | solution.py:18
  44.8 48.7 %all-gather.2.cloned.1.call-done = bf16[4,256,1024]{1,2,0:T(8,128)(2,1)} async-done(((bf16[4,256,16]{1,2,0:T(8,128)(2,1)}), bf16[4,256,1024]{1,2,0:T(8,128)(2,1)}) %all-gather.2.cloned.1.call-update) | async-done | bytes 2097168 | tf_op jit(solution)/shard_map/all_gather | solution.py:46
  93.5 3.7 convert_bitcast_fusion
  97.1 13.3 %copy.69 = bf16[2,32,4,4,1024]{1,3,0,2,4:T(4,128)(2,1)} copy(bf16[2,32,4,4,1024]{4,1,3,0,2:T(8,128)(2,1)} %convert_bitcast_fusion) | data formatting | bytes 4194304 | tf_op jit(solution)/shard_map/convert_element_type | solution.py:49
  110.4 13.7 %reshape.210 = bf16[64,2,8192]{2,1,0:T(2,128)(2,1)} reshape(bf16[1024,4,2,4,32]{4,3,2,1,0:T(4,128)(2,1)} %bitcast.106) | data formatting | bytes 4194304
  124.1 63.1 %all_to_all.74 = bf16[64,2,8192]{2,1,0:T(2,128)(2,1)} all-to-all(bf16[64,2,8192]{2,1,0:T(2,128)(2,1)} %reshape.210), channel_id=1, replica_groups=mesh['ta'=4,'pa'=64] {'pa'}, dimensions={0} | all-to-all | bytes 4194304 | tf_op jit(solution)/shard_map/all_to_all | solution.py:56
  187.2 13.3 %reshape.211 = bf16[1024,4,2,4,32]{4,3,2,1,0:T(4,128)(2,1)} reshape(bf16[64,2,8192]{2,1,0:T(2,128)(2,1)} %all_to_all.74) | data formatting | bytes 4194304
  200.4 9.8 %copy.70 = bf16[2,32,4,4,1024]{1,4,3,2,0:T(8,128)(2,1)} copy(bf16[2,32,4,4,1024]{1,3,0,2,4:T(4,128)(2,1)} %bitcast.107) | data formatting | bytes 4194304 | tf_op jit(solution)/shard_map/all_to_all | solution.py:56
  210.3 9.1 %copy.71 = bf16[2,32,4,64,4,16]{1,5,4,3,2,0:T(8,128)(2,1)} copy(bf16[2,32,4,64,4,16]{1,5,3,4,2,0:T(8,128)(2,1)} %bitcast.110) | data formatting | bytes 4194304 | tf_op jit(solution)/shard_map/all_to_all | solution.py:56
  219.4 11.9 %copy.72 = bf16[2,32,4,256,16]{3,4,1,0,2:T(8,128)(2,1)} copy(bf16[2,32,4,256,16]{1,4,3,2,0:T(8,128)(2,1)} %bitcast.108) | data formatting | bytes 4194304 | tf_op jit(solution)/shard_map/all_to_all | solution.py:56
  231.3 4.6 convolution_bitcast_fusion
  243.1 5.1 %copy.73 = bf16[32,1024,16]{0,2,1:T(8,128)(2,1)} copy(bf16[32,1024,16]{1,2,0:T(8,128)(2,1)S(1)} %fusion.28) | data formatting | bytes 2097152 | tf_op jit(solution)/shard_map/convert_element_type | solution.py:63
  248.2 6.4 %reshape.212 = bf16[64,2,4096]{2,1,0:T(2,128)(2,1)S(1)} reshape(bf16[1024,16,32]{2,1,0:T(8,128)(2,1)} %bitcast.113) | data formatting | bytes 2097152
  254.6 33.4 %all_to_all.75 = bf16[64,2,4096]{2,1,0:T(2,128)(2,1)} all-to-all(bf16[64,2,4096]{2,1,0:T(2,128)(2,1)S(1)} %reshape.212), channel_id=1, replica_groups=mesh['ta'=4,'pa'=64] {'pa'}, dimensions={0} | all-to-all | bytes 2097152 | tf_op jit(solution)/shard_map/all_to_all | solution.py:64
  288.0 6.5 %reshape.213 = bf16[1024,16,32]{2,1,0:T(8,128)(2,1)} reshape(bf16[64,2,4096]{2,1,0:T(2,128)(2,1)} %all_to_all.75) | data formatting | bytes 2097152
  294.5 5.2 %copy.74 = bf16[32,16,64,16]{0,3,2,1:T(8,128)(2,1)} copy(bf16[32,16,64,16]{0,3,1,2:T(8,128)(2,1)} %bitcast.117) | data formatting | bytes 2097152 | tf_op jit(solution)/shard_map/all_to_all | solution.py:64
  299.8 4.0 copy.75
  306.0 7.4 %copy.76 = bf16[32,16,1024]{0,1,2:T(8,128)(2,1)} copy(bf16[32,16,1024]{2,1,0:T(8,128)(2,1)} %fusion.25) | data formatting | bytes 2097152 | tf_op jit(solution)/shard_map/convert_element_type | solution.py:67
  313.4 6.4 %reshape.214 = bf16[64,2,4096]{2,1,0:T(2,128)(2,1)S(1)} reshape(bf16[1024,16,32]{2,1,0:T(8,128)(2,1)} %bitcast.114) | data formatting | bytes 2097152
  319.8 29.8 %all_to_all.76 = bf16[64,2,4096]{2,1,0:T(2,128)(2,1)S(1)} all-to-all(bf16[64,2,4096]{2,1,0:T(2,128)(2,1)S(1)} %reshape.214), channel_id=1, replica_groups=mesh['ta'=4,'pa'=64] {'pa'}, dimensions={0} | all-to-all | bytes 2097152 | tf_op jit(solution)/shard_map/all_to_all | solution.py:68
  349.6 3.5 reshape.215
  353.1 5.2 %copy.77 = bf16[32,16,1024]{2,1,0:T(8,128)(2,1)S(1)} copy(bf16[32,16,1024]{0,1,2:T(8,128)(2,1)} %bitcast.115) | data formatting | bytes 2097152 | tf_op jit(solution)/shard_map/all_to_all | solution.py:68
  358.4 4.2 copy.78
  362.6 7.8 %copy.79 = f32[32,64,16,16]{0,3,2,1:T(8,128)} copy(f32[32,64,16,16]{0,3,1,2:T(8,128)} %bitcast.111) | data formatting | bytes 4194304 | tf_op jit(solution)/shard_map/convert_element_type | solution.py:69
  370.4 6.8 %copy.80 = f32[32,1024,16]{1,2,0:T(8,128)} copy(f32[32,1024,16]{0,2,1:T(8,128)} %bitcast.109) | data formatting | bytes 4194304 | tf_op jit(solution)/shard_map/convert_element_type | solution.py:69
  377.2 5.2 %fusion.31 = bf16[32,4,256,16]{2,3,0,1:T(8,128)(2,1)S(1)} fusion(bf16[4,256,1024]{1,2,0:T(8,128)(2,1)S(1)} %copy-done.3, f32[2,32,4,1024,16]{3,4,1,0,2:T(8,128)} %copy-done.2, f32[32,1024,16]{1,2,0:T(8,128)} %copy.80), kind=kOutput, calls=%fused_computation.26 | convolution fusion | flops 1080557568 | bytes 13631488 | tf_op jit(solution)/shard_map/kip,tkpq->tkiq/dot_general | solution.py:70
  382.5 7.5 %copy.81 = bf16[32,4,256,16]{0,3,1,2:T(8,128)(2,1)} copy(bf16[32,4,256,16]{2,3,0,1:T(8,128)(2,1)S(1)} %fusion.31) | data formatting | bytes 2097152 | tf_op jit(solution)/shard_map/convert_element_type | solution.py:72
  389.9 7.3 %reshape.216 = bf16[64,2,4096]{2,1,0:T(2,128)(2,1)} reshape(bf16[256,4,16,32]{3,2,1,0:T(8,128)(2,1)} %bitcast.116) | data formatting | bytes 2097152
  397.2 6.4 %all-to-all-start.4 = ((bf16[64,2,4096]{2,1,0:T(2,128)(2,1)}), bf16[64,2,4096]{2,1,0:T(2,128)(2,1)S(1)}, u32[]{:S(2)}, u32[]{:S(2)}) async-start(bf16[64,2,4096]{2,1,0:T(2,128)(2,1)} %reshape.216), calls=%async_computation.4 | async-start | bytes 2097152 | tf_op jit(solution)/shard_map/all_to_all | solution.py:75
  403.6 21.3 %all-to-all-done.4 = bf16[64,2,4096]{2,1,0:T(2,128)(2,1)S(1)} async-done(((bf16[64,2,4096]{2,1,0:T(2,128)(2,1)}), bf16[64,2,4096]{2,1,0:T(2,128)(2,1)S(1)}, u32[]{:S(2)}, u32[]{:S(2)}) %all-to-all-start.4) | async-done | bytes 1048608 | tf_op jit(solution)/shard_map/all_to_all | solution.py:75
  424.9 3.5 reshape.217
  435.0 36.9 %all_to_all.77 = bf16[4,64,4,4,256]{4,1,3,2,0:T(8,128)(2,1)} all-to-all(bf16[4,64,4,4,256]{4,1,3,2,0:T(8,128)(2,1)S(1)} %copy.85), channel_id=1, replica_groups=mesh['ta'=4,'pa'=64] {'ta'}, dimensions={0} | all-to-all | bytes 4194304 | tf_op jit(solution)/shard_map/all_to_all | solution.py:18
  (25 shorter events, 25.6 us)
Async XLA Ops:
  6.5 235.2 %copy-start = (bf16[1024,1024]{1,0:T(8,128)(2,1)S(1)}, bf16[1024,1024]{1,0:T(8,128)(2,1)}, u32[]{:S(2)}) copy-start(bf16[1024,1024]{1,0:T(8,128)(2,1)} %param.5) | copy-start | bytes 6291460
  6.5 86.9 %all-gather.2.cloned.1.call-start = ((), (), s32[]{:S(2)}) async-start(), calls=%async_computation.6 | async-start | bytes 2129920 | tf_op jit(solution)/shard_map/all_gather | solution.py:46
  235.9 5.8 %copy-start.2 = (f32[2,32,4,1024,16]{3,4,1,0,2:T(8,128)}, f32[2,32,4,1024,16]{3,4,1,0,2:T(8,128)S(1)}, u32[]{:S(2)}) copy-start(f32[2,32,4,1024,16]{3,4,1,0,2:T(8,128)S(1)} %convolution_bitcast_fusion) | copy-start | bytes 50331652
  370.4 6.8 %copy-start.3 = (bf16[4,256,1024]{1,2,0:T(8,128)(2,1)S(1)}, bf16[4,256,1024]{1,2,0:T(8,128)(2,1)}, u32[]{:S(2)}) copy-start(bf16[4,256,1024]{1,2,0:T(8,128)(2,1)} %all-gather.2.cloned.1.call-done) | copy-start | bytes 6291460
  397.2 27.7 %all-to-all-start.4 = ((bf16[64,2,4096]{2,1,0:T(2,128)(2,1)}), bf16[64,2,4096]{2,1,0:T(2,128)(2,1)S(1)}, u32[]{:S(2)}, u32[]{:S(2)}) async-start(bf16[64,2,4096]{2,1,0:T(2,128)(2,1)} %reshape.216), calls=%async_computation.4 | async-start | bytes 2097152 | tf_op jit(solution)/shard_map/all_to_all | solution.py:75
  435.0 40.1 %copy-start.1 = (bf16[1024,1024]{1,0:T(8,128)(2,1)S(1)}, bf16[1024,1024]{1,0:T(8,128)(2,1)}, u32[]{:S(2)}) copy-start(bf16[1024,1024]{1,0:T(8,128)(2,1)} %param.5) | copy-start | bytes 6291460
Sparse Core Ops, SparseCore 0:
  10.5 82.9 all-gather.1
where the time goes:
time: 490 us; the launch traced here: 482 us
  blocking collectives  195 us (40%)
  local copies, waits for them, and re-layouts  166 us (34%)
  waiting for transfers between devices  70.7 us (14%)
  matrix products  23.1 us (5%)
  between operations  13.8 us (3%)
  other arithmetic  7.16 us (1%)
  starting transfers between devices  6.38 us (1%)
    all_to_all x2, blocking collectives, summed_on_arrival(): lax.all_to_all(blocks, axis, split_axis=0, concat_axis=0, tiled=True)  68.6 us
    unnamed x16, local copies, waits for them, and re-layouts  63.9 us
    all_to_all x1, blocking collectives, local(): lax.all_to_all(half_piece, 'pa', split_axis=4, concat_axis=3, tiled=True)  63.1 us
    all_gather x1, waiting for transfers between devices, local(): piece = lax.all_gather(colloc, 'pa', axis=2, tiled=True)  48.7 us
    all_to_all x1, blocking collectives, local(): lax.all_to_all(mixed, 'pa', split_axis=1, concat_axis=2, tiled=True)  33.4 us
    all_to_all x3, local copies, waits for them, and re-layouts, local(): lax.all_to_all(half_piece, 'pa', split_axis=4, concat_axis=3, tiled=True)  30.9 us
    all_to_all x1, blocking collectives, local(): lax.all_to_all(screened_rows, 'pa', split_axis=2, concat_axis=1, tiled=True)  29.8 us
    all_to_all x1, waiting for transfers between devices, local(): lax.all_to_all(outer, 'pa', split_axis=2, concat_axis=3, tiled=True)  21.3 us
  transfers between devices with their start and end apart: 2, of which 2 were waited for; matrix products, arithmetic and copies ran while one was open for 1% of the time, Pallas kernels for 0%

commit v1 on v0

v1 whole, which is shorter than its diff:
```python
import functools

import jax
import jax.numpy as jnp
from jax import lax
from jax.experimental import pallas as pl
from jax.experimental.pallas import tpu as pltpu
from jax.sharding import PartitionSpec as P

NFREQ = 128
NPTS = 1024
NORB = 256
bf16 = jnp.bfloat16
f32 = jnp.float32

CORE_SWAP = [(0, 1), (1, 0), (2, 3), (3, 2)]
CHIP_SWAP = [(0, 2), (2, 0), (1, 3), (3, 1)]
NT = ((1,), (1,))
TN = ((0,), (0,))


def x_shift(step):
    return [(i, (i + 16 * step) % 64) for i in range(64)]


def half_tables():
    freq = jnp.arange(NFREQ, dtype=f32)
    times = jnp.arange(NFREQ // 2, dtype=f32)
    phase = jnp.pi * (2.0 * freq[None, :] + 1.0) * (times[:, None] + 0.5) / NFREQ
    scale = 1.0 / jnp.sqrt(f32(NFREQ))
    return jnp.cos(phase) * scale, jnp.sin(phase) * scale


def dot(a, b, dims=((1,), (0,))):
    return lax.dot_general(a, b, (dims, ((), ())), preferred_element_type=f32)


def pair_kernel(TP, TQ, TW, x_ref, g_ref, core_ref, out_ref, t_ref, bub_ref, mix_ref, own_ref, tmp_ref):
    def p_step(pb, _):
        rows = pl.ds(pl.multiple_of(pb * TP, TP), TP)
        for k in range(4):
            xk = x_ref[k, rows, :]
            for s in range(2):
                t_ref[s * 4 + k] = dot(xk, g_ref[s, k]).astype(bf16)

        def q_step(qb, _):
            cols = pl.ds(pl.multiple_of(qb * TQ, TQ), TQ)
            acc = None
            for k in range(4):
                xq = x_ref[k, cols, :]
                v = dot(t_ref[k], xq, NT)
                if k < 2:
                    own_ref[k, rows, cols] = v
                w = dot(t_ref[4 + k], xq, NT)
                term = v * v - w * w
                acc = term if acc is None else acc + term
            bub_ref[rows, cols] = (acc * 0.25).astype(bf16)
            return 0

        lax.fori_loop(0, NPTS // TQ, q_step, 0)
        return 0

    lax.fori_loop(0, NPTS // TP, p_step, 0)

    def mixed_step(i, _):
        rows = pl.ds(pl.multiple_of(i * TW, TW), TW)
        mix_ref[rows, :] = dot(core_ref[rows, :], bub_ref[...]).astype(bf16)
        return 0

    lax.fori_loop(0, NPTS // TW, mixed_step, 0)

    def source_step(i, _):
        rows = pl.ds(pl.multiple_of(i * TW, TW), TW)
        w = dot(mix_ref[rows, :], core_ref[...])
        for k in range(2):
            source = (own_ref[k, rows, :] * w).astype(bf16)
            tmp_ref[k, rows, :] = dot(source, x_ref[k]).astype(bf16)
        return 0

    lax.fori_loop(0, NPTS // TW, source_step, 0)
    for k in range(2):
        out_ref[k] = dot(x_ref[k], tmp_ref[k], TN).astype(bf16)


def pair_call(x, g, core, TP=1024, TQ=256, TW=512):
    vm = pl.BlockSpec(memory_space=pltpu.VMEM)
    return pl.pallas_call(
        functools.partial(pair_kernel, TP, TQ, TW),
        out_shape=jax.ShapeDtypeStruct((2, NORB, NORB), bf16),
        in_specs=[vm] * 3,
        out_specs=vm,
        scratch_shapes=[
            pltpu.VMEM((8, TP, NORB), bf16),
            pltpu.VMEM((NPTS, NPTS), bf16),
            pltpu.VMEM((NPTS, NPTS), bf16),
            pltpu.VMEM((2, NPTS, NPTS), f32),
            pltpu.VMEM((2, NPTS, NORB), bf16),
        ],
        compiler_params=pltpu.CompilerParams(vmem_limit_bytes=48 << 20),
        cost_estimate=pl.CostEstimate(flops=11_000_000_000, bytes_accessed=6 << 20, transcendentals=0),
    )(x, g, core)


def local(green_freq, colloc, core):
    ta = lax.axis_index("ta")
    c = ta % 2
    xpos = lax.axis_index("pa") // 16
    cosine, sine = half_tables()
    table = jnp.where(ta < 2, cosine, sine)
    own_w = lax.dynamic_slice_in_dim(table, c * 64, 64, 1)
    other_w = lax.dynamic_slice_in_dim(table, 64 - c * 64, 64, 1)

    gf = green_freq.reshape(64, 2, 8, NORB)
    mine = lax.dynamic_index_in_dim(gf, c, 1, keepdims=False)
    theirs = lax.dynamic_index_in_dim(gf, 1 - c, 1, keepdims=False)
    arrived = lax.ppermute(theirs, "ta", CORE_SWAP)
    part = jnp.einsum("uw,wrj->urj", own_w, mine.astype(f32), precision=lax.Precision.HIGHEST)
    part += jnp.einsum("uw,wrj->urj", other_w, arrived.astype(f32), precision=lax.Precision.HIGHEST)
    part = part.astype(bf16)

    xt = jnp.swapaxes(colloc, 1, 2).reshape(2, 4, 8, NORB)
    xt = lax.dynamic_index_in_dim(xt, c, 0, keepdims=False)
    xmsg = jnp.broadcast_to(xt[:, None], (4, 16, 8, NORB)).reshape(64, 8, NORB)
    got = lax.all_to_all(jnp.concatenate([part, xmsg], 1), "pa", 0, 0, tiled=True)
    green = got[:, :8].reshape(64, 2, 4, NORB).swapaxes(0, 1).reshape(2, NORB, NORB)
    xpart = got[:, 8:]

    other = lax.ppermute(green, "ta", CHIP_SWAP)
    pieces = [xpart] + [lax.ppermute(xpart, "pa", x_shift(s)) for s in (1, 2, 3)]
    blocks = jnp.zeros((4, 64, 8, NORB), bf16)
    for s in range(4):
        blocks = lax.dynamic_update_slice_in_dim(blocks, pieces[s][None], (xpos - s) % 4, 0)
    xown = blocks.reshape(2, 2, 64, 8, NORB).swapaxes(1, 2).reshape(2, NPTS, NORB)

    gown = jnp.stack([green, other])
    gnext = lax.ppermute(gown, "ta", CORE_SWAP)
    xnext = lax.ppermute(xown, "ta", CORE_SWAP)
    out = pair_call(jnp.concatenate([xown, xnext], 0), jnp.concatenate([gown, gnext], 1), core)

    msg = out.reshape(2, 64, 4, NORB).swapaxes(0, 1).reshape(64, 8, NORB)
    back = lax.all_to_all(msg, "pa", 0, 0, tiled=True)
    back_next = lax.ppermute(back, "ta", CORE_SWAP)
    first = jnp.where(c == 0, back, back_next)
    second = jnp.where(c == 0, back_next, back)
    both = jnp.concatenate([first, second], 1)
    final = own_w * jnp.where(ta < 2, 2.0, -2.0)
    result = jnp.einsum("uw,urj->wrj", final, both.astype(f32), precision=lax.Precision.HIGHEST)
    return result.astype(bf16).reshape(64, 4, 4, NORB)


def solution(mesh):
    return jax.shard_map(
        local,
        mesh=mesh,
        in_specs=(P("ta", None, "pa", None), P(None, None, "pa"), P()),
        out_specs=P("ta", None, "pa", None),
        check_vma=False,
    )
```

time: 490 us -> 98.2 us (0.20); the launches traced: 482 us -> 98 us
  local copies, waits for them, and re-layouts: 166 us -> 4.99 us
  blocking collectives: 195 us -> 51.3 us
  waiting for transfers between devices: 70.7 us -> 13.9 us
  matrix products: 23.1 us -> 1.55 us
  between operations: 13.8 us -> 0.36 us
  Pallas kernels: 0 us -> 13.1 us
  other arithmetic: 7.16 us -> 0.67 us
  starting transfers between devices: 6.38 us -> 12.1 us
    all_to_all x5 -> x2, blocking collectives: 195 us -> 51.3 us  [the longest x1 31.5 us: local(): lax.all_to_all(jnp.concatenate([part, xmsg], 1), 'pa', 0, 0, tiled=True)]
    unnamed x16 -> x4, local copies, waits for them, and re-layouts: 63.9 us -> 1.39 us
    convert_element_type x7 -> x0, local copies, waits for them, and re-layouts: 52.1 us -> none  [the longest x3 18.8 us: local(): screened.astype(jnp.float32)[:, None]]
    all_gather x1 -> x0, waiting for transfers between devices: 48.7 us -> none  [local(): piece = lax.all_gather(colloc, 'pa', axis=2, tiled=True)]
    all_to_all x7 -> x1, local copies, waits for them, and re-layouts: 48.6 us -> 0.05 us  [local(): back = lax.all_to_all(msg, 'pa', 0, 0, tiled=True)]
    dot_general x8 -> x3, matrix products: 23.1 us -> 1.55 us  [the longest x1 0.7 us: local(): jnp.einsum('uw,urj->wrj', final, both.astype(f32), precision=lax.Precisio...]
    all_to_all x1 -> x0, waiting for transfers between devices: 21.3 us -> none  [local(): lax.all_to_all(outer, 'pa', split_axis=2, concat_axis=3, tiled=True)]
    ppermute x0 -> x8, waiting for transfers between devices: none -> 13.9 us  [the longest x3 9.71 us: local(): lax.ppermute(xpart, 'pa', x_shift(s))]
  transfers between devices with their start and end apart: 2 -> 8, of which waited for: 2 -> 6; matrix products, arithmetic and copies ran while one was open for 1% -> 1% of each run, Pallas kernels for 0% -> 0%
where the time goes in v1:
time: 98.2 us; the launch traced here: 98 us
  blocking collectives  51.3 us (52%)
  waiting for transfers between devices  13.9 us (14%)
  Pallas kernels  13.1 us (13%)
  starting transfers between devices  12.1 us (12%)
  local copies, waits for them, and re-layouts  4.99 us (5%)
  matrix products  1.55 us (2%)
    all_to_all x1, blocking collectives, local(): lax.all_to_all(jnp.concatenate([part, xmsg], 1), 'pa', 0, 0, tiled=True)  31.5 us
    all_to_all x1, blocking collectives, local(): back = lax.all_to_all(msg, 'pa', 0, 0, tiled=True)  19.8 us
    pallas_call x1, Pallas kernels, pair_call(): pl.pallas_call(functools.partial(pair_kernel, TP, TQ, TW), out_shape=jax....  13.1 us
    ppermute x3, waiting for transfers between devices, local(): lax.ppermute(xpart, 'pa', x_shift(s))  9.71 us
    ppermute x1, starting transfers between devices, local(): arrived = lax.ppermute(theirs, 'ta', CORE_SWAP)  3.29 us
    ppermute x3, starting transfers between devices, local(): lax.ppermute(xpart, 'pa', x_shift(s))  2.66 us
    ppermute x1, waiting for transfers between devices, local(): gnext = lax.ppermute(gown, 'ta', CORE_SWAP)  2.62 us
    ppermute x1, starting transfers between devices, local(): back_next = lax.ppermute(back, 'ta', CORE_SWAP)  2.4 us
  transfers between devices with their start and end apart: 8, of which 6 were waited for; matrix products, arithmetic and copies ran while one was open for 1% of the time, Pallas kernels for 0%

profile of v1, /device:TPU:1, one launch (start us, length us, event | category | flops | bytes accessed | tf_op | source)
XLA Modules:
  0.0 98.0 jit_solution(13016491099598972625)
XLA Ops:
  0.0 1.2 %copy.36 = bf16[64,4,4,256]{3,0,2,1:T(8,128)(2,1)S(1)} copy(bf16[64,4,4,256]{3,2,1,0:T(4,128)(2,1)} %param.3) | data formatting | bytes 1048576 | tf_op jit(solution)/shard_map/reshape | solution.py:113
  1.3 3.3 %collective-permute-start = (bf16[64,8,256]{2,0,1:T(8,128)(2,1)S(1)}, bf16[64,8,256]{2,0,1:T(8,128)(2,1)S(1)}, u32[]{:S(2)}, u32[]{:S(2)}) collective-permute-start(bf16[64,8,256]{2,0,1:T(8,128)(2,1)S(1)} %dynamic-slice_bitcast_fusion), channel_id=1, source_target_pairs={{0,64},{64,0},{128,192},{192,128},{1,65},{65,1},{129,193},{193,129... | collective-permute-start | bytes 786440 | tf_op jit(solution)/shard_map/ppermute | solution.py:116
  4.6 0.2 multiply_select_fusion
  4.8 0.4 fusion.4
  5.3 0.4 collective-permute-done
  5.7 0.4 fusion
  6.2 0.3 copy.25
  6.5 31.5 %all_to_all.10 = bf16[64,16,256]{2,1,0:T(8,128)(2,1)S(1)} all-to-all(bf16[64,16,256]{2,1,0:T(8,128)(2,1)S(1)} %copy.25), channel_id=1, replica_groups=mesh['ta'=4,'pa'=64] {'pa'}, dimensions={0} | all-to-all | bytes 1048576 | tf_op jit(solution)/shard_map/all_to_all | solution.py:124
  38.1 0.1 collective-permute-start.1
  38.3 1.5 %collective-permute-start.2 = (bf16[64,8,256]{2,1,0:T(8,128)(2,1)S(1)}, bf16[64,8,256]{2,1,0:T(8,128)(2,1)S(1)}, u32[]{:S(2)}, u32[]{:S(2)}) collective-permute-start(bf16[64,8,256]{2,1,0:T(8,128)(2,1)S(1)} %get-tuple-element.8), channel_id=1, source_target_pairs={{0,32},{1,33},{2,34},{3,35},{4,36},{5,37},{6,38},{7,39},{8,40},{9,... | collective-permute-start | bytes 786440 | tf_op jit(solution)/shard_map/ppermute | solution.py:129
  39.8 1.0 %collective-permute-start.3 = (bf16[64,8,256]{2,1,0:T(8,128)(2,1)S(1)}, bf16[64,8,256]{2,1,0:T(8,128)(2,1)S(1)}, u32[]{:S(2)}, u32[]{:S(2)}) collective-permute-start(bf16[64,8,256]{2,1,0:T(8,128)(2,1)S(1)} %get-tuple-element.8), channel_id=1, source_target_pairs={{0,48},{1,49},{2,50},{3,51},{4,52},{5,53},{6,54},{7,55},{8,56},{9,... | collective-permute-start | bytes 786440 | tf_op jit(solution)/shard_map/ppermute | solution.py:129
  40.9 0.1 copy.40
  41.0 0.1 reshape.52
  41.1 1.1 %collective-permute-start.5 = (bf16[2,256,256]{2,1,0:T(8,128)(2,1)S(1)}, bf16[2,256,256]{2,1,0:T(8,128)(2,1)S(1)}, u32[]{:S(2)}, u32[]{:S(2)}) collective-permute-start(bf16[2,256,256]{2,1,0:T(8,128)(2,1)S(1)} %reshape.52), channel_id=1, source_target_pairs={{0,128},{128,0},{64,192},{192,64},{1,129},{129,1},{65,193},{193,65... | collective-permute-start | bytes 786440 | tf_op jit(solution)/shard_map/ppermute | solution.py:128
  42.2 0.1 broadcast_in_dim.25
  42.3 5.0 %collective-permute-done.1 = bf16[64,8,256]{2,1,0:T(8,128)(2,1)S(1)} collective-permute-done((bf16[64,8,256]{2,1,0:T(8,128)(2,1)S(1)}, bf16[64,8,256]{2,1,0:T(8,128)(2,1)S(1)}, u32[]{:S(2)}, u32[]{:S(2)}) %collective-permute-start.1) | collective-permute-done | bytes 262176 | tf_op jit(solution)/shard_map/ppermute | solution.py:129
  47.4 1.5 %collective-permute-done.2 = bf16[64,8,256]{2,1,0:T(8,128)(2,1)S(1)} collective-permute-done((bf16[64,8,256]{2,1,0:T(8,128)(2,1)S(1)}, bf16[64,8,256]{2,1,0:T(8,128)(2,1)S(1)}, u32[]{:S(2)}, u32[]{:S(2)}) %collective-permute-start.2) | collective-permute-done | bytes 262176 | tf_op jit(solution)/shard_map/ppermute | solution.py:129
  48.9 3.1 %collective-permute-done.3 = bf16[64,8,256]{2,1,0:T(8,128)(2,1)S(1)} collective-permute-done((bf16[64,8,256]{2,1,0:T(8,128)(2,1)S(1)}, bf16[64,8,256]{2,1,0:T(8,128)(2,1)S(1)}, u32[]{:S(2)}, u32[]{:S(2)}) %collective-permute-start.3) | collective-permute-done | bytes 262176 | tf_op jit(solution)/shard_map/ppermute | solution.py:129
  52.1 0.1 copy.26
  52.2 2.4 %collective-permute-start.4 = (bf16[2,1024,256]{2,1,0:T(8,128)(2,1)S(1)}, bf16[2,1024,256]{2,1,0:T(8,128)(2,1)S(1)}, u32[]{:S(2)}, u32[]{:S(2)}) collective-permute-start(bf16[2,1024,256]{2,1,0:T(8,128)(2,1)S(1)} %bitcast.42), channel_id=1, source_target_pairs={{0,64},{64,0},{128,192},{192,128},{1,65},{65,1},{129,193},{193,129... | collective-permute-start | bytes 3145736 | tf_op jit(solution)/shard_map/ppermute | solution.py:137
  54.7 0.3 collective-permute-start.6
  55.0 2.6 %collective-permute-done.6 = bf16[2,2,256,256]{3,2,1,0:T(8,128)(2,1)S(1)} collective-permute-done((bf16[2,2,256,256]{3,2,1,0:T(8,128)(2,1)S(1)}, bf16[2,2,256,256]{3,2,1,0:T(8,128)(2,1)S(1)}, u32[]{:S(2)}, u32[]{:S(2)}) %collective-permute-start.6) | collective-permute-done | bytes 524320 | tf_op jit(solution)/shard_map/ppermute | solution.py:136
  57.6 0.1 pad_maximum_fusion.1.g_ref
  57.7 0.2 pad_maximum_fusion.x_ref
  57.9 1.4 %copy-done.1 = bf16[1024,1024]{1,0:T(8,128)(2,1)S(1)} copy-done((bf16[1024,1024]{1,0:T(8,128)(2,1)S(1)}, bf16[1024,1024]{1,0:T(8,128)(2,1)}, u32[]{:S(2)}) %copy-start.1) | copy-done | bytes 2097176
  59.3 13.1 %shard_map.37 = bf16[2,256,256]{2,1,0:T(8,128)(2,1)S(1)} custom-call(bf16[4,1024,256]{2,1,0:T(8,128)(2,1)S(1)} %pad_maximum_fusion.x_ref, bf16[2,4,256,256]{3,2,1,0:T(8,128)(2,1)S(1)} %pad_maximum_fusion.1.g_ref, bf16[1024,1024]{1,0:T(8,128)(2,1)S(1)} %copy-done.1), custom_call_target="tpu_custom_call" | custom-call | flops 11000000512 | bytes 6291456 | tf_op jit(solution)/shard_map/pallas_call | solution.py:87
  72.5 0.1 copy.28
  72.6 19.8 %all_to_all.11 = bf16[64,8,256]{2,1,0:T(8,128)(2,1)S(1)} all-to-all(bf16[64,8,256]{2,1,0:T(8,128)(2,1)S(1)} %reshape.54), channel_id=1, replica_groups=mesh['ta'=4,'pa'=64] {'pa'}, dimensions={0} | all-to-all | bytes 524288 | tf_op jit(solution)/shard_map/all_to_all | solution.py:141
  92.5 2.4 %collective-permute-start.7 = (bf16[64,8,256]{2,0,1:T(8,128)(2,1)S(1)}, bf16[64,8,256]{2,0,1:T(8,128)(2,1)S(1)}, u32[]{:S(2)}, u32[]{:S(2)}) collective-permute-start(bf16[64,8,256]{2,0,1:T(8,128)(2,1)S(1)} %copy.30), channel_id=1, source_target_pairs={{0,64},{64,0},{128,192},{192,128},{1,65},{65,1},{129,193},{193,129... | collective-permute-start | bytes 786440 | tf_op jit(solution)/shard_map/ppermute | solution.py:142
  94.9 1.2 %collective-permute-done.7 = bf16[64,8,256]{2,0,1:T(8,128)(2,1)S(1)} collective-permute-done((bf16[64,8,256]{2,0,1:T(8,128)(2,1)S(1)}, bf16[64,8,256]{2,0,1:T(8,128)(2,1)S(1)}, u32[]{:S(2)}, u32[]{:S(2)}) %collective-permute-start.7) | collective-permute-done | bytes 262176 | tf_op jit(solution)/shard_map/ppermute | solution.py:142
  96.1 0.7 convolution_convert_fusion
  96.8 1.2 %copy.33 = bf16[64,4,4,256]{3,2,1,0:T(4,128)(2,1)} copy(bf16[64,4,4,256]{3,0,2,1:T(8,128)(2,1)S(1)} %bitcast.46) | data formatting | bytes 1048576 | tf_op jit(solution)/shard_map/reshape | solution.py:148
  (24 shorter events, 0.7 us)
Async XLA Ops:
  0.0 4.6 %copy-start = (bf16[4,256,16]{1,2,0:T(8,128)(2,1)S(1)}, bf16[4,256,16]{1,2,0:T(8,128)(2,1)}, u32[]{:S(2)}) copy-start(bf16[4,256,16]{1,2,0:T(8,128)(2,1)} %param.4) | copy-start | bytes 98308
  1.3 4.5 %collective-permute-start = (bf16[64,8,256]{2,0,1:T(8,128)(2,1)S(1)}, bf16[64,8,256]{2,0,1:T(8,128)(2,1)S(1)}, u32[]{:S(2)}, u32[]{:S(2)}) collective-permute-start(bf16[64,8,256]{2,0,1:T(8,128)(2,1)S(1)} %dynamic-slice_bitcast_fusion), channel_id=1, source_target_pairs={{0,64},{64,0},{128,192},{192,128},{1,65},{65,1},{129,193},{193,129... | collective-permute-start | bytes 786440 | tf_op jit(solution)/shard_map/ppermute | solution.py:116
  38.1 9.2 %collective-permute-start.1 = (bf16[64,8,256]{2,1,0:T(8,128)(2,1)S(1)}, bf16[64,8,256]{2,1,0:T(8,128)(2,1)S(1)}, u32[]{:S(2)}, u32[]{:S(2)}) collective-permute-start(bf16[64,8,256]{2,1,0:T(8,128)(2,1)S(1)} %get-tuple-element.8), channel_id=1, source_target_pairs={{0,16},{1,17},{2,18},{3,19},{4,20},{5,21},{6,22},{7,23},{8,24},{9,... | collective-permute-start | bytes 786440 | tf_op jit(solution)/shard_map/ppermute | solution.py:129
  38.3 10.6 %collective-permute-start.2 = (bf16[64,8,256]{2,1,0:T(8,128)(2,1)S(1)}, bf16[64,8,256]{2,1,0:T(8,128)(2,1)S(1)}, u32[]{:S(2)}, u32[]{:S(2)}) collective-permute-start(bf16[64,8,256]{2,1,0:T(8,128)(2,1)S(1)} %get-tuple-element.8), channel_id=1, source_target_pairs={{0,32},{1,33},{2,34},{3,35},{4,36},{5,37},{6,38},{7,39},{8,40},{9,... | collective-permute-start | bytes 786440 | tf_op jit(solution)/shard_map/ppermute | solution.py:129
  39.8 12.2 %collective-permute-start.3 = (bf16[64,8,256]{2,1,0:T(8,128)(2,1)S(1)}, bf16[64,8,256]{2,1,0:T(8,128)(2,1)S(1)}, u32[]{:S(2)}, u32[]{:S(2)}) collective-permute-start(bf16[64,8,256]{2,1,0:T(8,128)(2,1)S(1)} %get-tuple-element.8), channel_id=1, source_target_pairs={{0,48},{1,49},{2,50},{3,51},{4,52},{5,53},{6,54},{7,55},{8,56},{9,... | collective-permute-start | bytes 786440 | tf_op jit(solution)/shard_map/ppermute | solution.py:129
  41.1 13.5 %collective-permute-start.5 = (bf16[2,256,256]{2,1,0:T(8,128)(2,1)S(1)}, bf16[2,256,256]{2,1,0:T(8,128)(2,1)S(1)}, u32[]{:S(2)}, u32[]{:S(2)}) collective-permute-start(bf16[2,256,256]{2,1,0:T(8,128)(2,1)S(1)} %reshape.52), channel_id=1, source_target_pairs={{0,128},{128,0},{64,192},{192,64},{1,129},{129,1},{65,193},{193,65... | collective-permute-start | bytes 786440 | tf_op jit(solution)/shard_map/ppermute | solution.py:128
  52.2 5.5 %collective-permute-start.4 = (bf16[2,1024,256]{2,1,0:T(8,128)(2,1)S(1)}, bf16[2,1024,256]{2,1,0:T(8,128)(2,1)S(1)}, u32[]{:S(2)}, u32[]{:S(2)}) collective-permute-start(bf16[2,1024,256]{2,1,0:T(8,128)(2,1)S(1)} %bitcast.42), channel_id=1, source_target_pairs={{0,64},{64,0},{128,192},{192,128},{1,65},{65,1},{129,193},{193,129... | collective-permute-start | bytes 3145736 | tf_op jit(solution)/shard_map/ppermute | solution.py:137
  54.7 2.9 %collective-permute-start.6 = (bf16[2,2,256,256]{3,2,1,0:T(8,128)(2,1)S(1)}, bf16[2,2,256,256]{3,2,1,0:T(8,128)(2,1)S(1)}, u32[]{:S(2)}, u32[]{:S(2)}) collective-permute-start(bf16[2,2,256,256]{3,2,1,0:T(8,128)(2,1)S(1)} %pad_maximum_fusion.3), channel_id=1, source_target_pairs={{0,64},{64,0},{128,192},{192,128},{1,65},{65,1},{129,193},{193,129... | collective-permute-start | bytes 1572872 | tf_op jit(solution)/shard_map/ppermute | solution.py:136
  57.7 1.6 %copy-start.1 = (bf16[1024,1024]{1,0:T(8,128)(2,1)S(1)}, bf16[1024,1024]{1,0:T(8,128)(2,1)}, u32[]{:S(2)}) copy-start(bf16[1024,1024]{1,0:T(8,128)(2,1)} %core_ref.1) | copy-start | bytes 6291460
  92.5 3.6 %collective-permute-start.7 = (bf16[64,8,256]{2,0,1:T(8,128)(2,1)S(1)}, bf16[64,8,256]{2,0,1:T(8,128)(2,1)S(1)}, u32[]{:S(2)}, u32[]{:S(2)}) collective-permute-start(bf16[64,8,256]{2,0,1:T(8,128)(2,1)S(1)} %copy.30), channel_id=1, source_target_pairs={{0,64},{64,0},{128,192},{192,128},{1,65},{65,1},{129,193},{193,129... | collective-permute-start | bytes 786440 | tf_op jit(solution)/shard_map/ppermute | solution.py:142

commit v2 on v1

v2 whole, which is shorter than its diff:
```python
import functools

import jax
import jax.numpy as jnp
from jax import lax
from jax.experimental import pallas as pl
from jax.experimental.pallas import tpu as pltpu
from jax.sharding import PartitionSpec as P


NFREQ = 128
NPTS = 1024
NORB = 256
bf16 = jnp.bfloat16
f32 = jnp.float32

CORE_SWAP = [(0, 1), (1, 0), (2, 3), (3, 2)]
CHIP_SWAP = [(0, 2), (2, 0), (1, 3), (3, 1)]
NT = ((1,), (1,))
TN = ((0,), (0,))


def square_pairs(step):
    def partner(v, core):
        return v ^ 1 if core == 0 else ((v + 1) ^ 1) - 1 & 3

    pairs = []
    for ta in range(4):
        for i in range(64):
            x, y, z = i // 16, (i // 4) % 4, i % 4
            x = partner(x, ta % 2) if step & 2 else x
            y = partner(y, ta % 2) if step & 1 else y
            pairs.append((ta * 64 + i, ta * 64 + x * 16 + y * 4 + z))
    return pairs


def half_tables():
    freq = jnp.arange(NFREQ, dtype=f32)
    times = jnp.arange(NFREQ // 2, dtype=f32)
    phase = jnp.pi * (2.0 * freq[None, :] + 1.0) * (times[:, None] + 0.5) / NFREQ
    scale = 1.0 / jnp.sqrt(f32(NFREQ))
    return jnp.cos(phase) * scale, jnp.sin(phase) * scale


def dot(a, b, dims=((1,), (0,))):
    return lax.dot_general(a, b, (dims, ((), ())), preferred_element_type=f32)


def points_of(x_ref, slots, kk, rows):
    return jnp.concatenate([x_ref[slots[2 * kk], rows, :], x_ref[slots[2 * kk + 1], rows, :]], axis=1)


def half_bubble(TQ, slots, x_ref, g_mine, g_else, t_ref, own_ref, emit):
    every = pl.ds(0, NPTS)
    for kk in range(2):
        xk = points_of(x_ref, slots, kk, every)
        t_ref[kk] = dot(xk, g_mine[kk]).astype(bf16)
        t_ref[2 + kk] = dot(xk, g_else[kk]).astype(bf16)

    def q_step(qb, _):
        cols = pl.ds(pl.multiple_of(qb * TQ, TQ), TQ)
        acc = None
        for kk in range(2):
            xq = points_of(x_ref, slots, kk, cols)
            v = dot(t_ref[kk], xq, NT)
            if own_ref is not None:
                own_ref[kk, :, cols] = v
            w = dot(t_ref[2 + kk], xq, NT)
            term = v * v - w * w
            acc = term if acc is None else acc + term
        emit(cols, acc)
        return 0

    lax.fori_loop(0, NPTS // TQ, q_step, 0)


def first_kernel(TQ, slot_ref, x_ref, g_mine, g_else, acc_ref, own_ref, t_ref):
    slots = [slot_ref[i] for i in range(4)]

    def emit(cols, acc):
        acc_ref[:, cols] = acc

    half_bubble(TQ, slots, x_ref, g_mine, g_else, t_ref, own_ref, emit)


def second_kernel(TQ, TW, slot_ref, x_own, x_next, g_mine, g_else, acc_ref, own_ref, core_ref, out_ref,
                  t_ref, bub_ref, mix_ref, tmp_ref):
    slots = [slot_ref[i] for i in range(4)]

    def emit(cols, acc):
        bub_ref[:, cols] = ((acc + acc_ref[:, cols]) * 0.25).astype(bf16)

    half_bubble(TQ, slots, x_next, g_mine, g_else, t_ref, None, emit)

    def mixed_step(i, _):
        rows = pl.ds(pl.multiple_of(i * TW, TW), TW)
        mix_ref[rows, :] = dot(core_ref[rows, :], bub_ref[...]).astype(bf16)
        return 0

    lax.fori_loop(0, NPTS // TW, mixed_step, 0)
    every = pl.ds(0, NPTS)

    def source_step(i, _):
        rows = pl.ds(pl.multiple_of(i * TW, TW), TW)
        w = dot(mix_ref[rows, :], core_ref[...])
        for kk in range(2):
            source = (own_ref[kk, rows, :] * w).astype(bf16)
            tmp_ref[kk, rows, :] = dot(source, points_of(x_own, slots, kk, every)).astype(bf16)
        return 0

    lax.fori_loop(0, NPTS // TW, source_step, 0)
    for kk in range(2):
        out_ref[kk] = dot(points_of(x_own, slots, kk, every), tmp_ref[kk], TN).astype(bf16)


VM = pl.BlockSpec(memory_space=pltpu.VMEM)
SM = pl.BlockSpec(memory_space=pltpu.SMEM)


def first_call(slots, x, g_mine, g_else, TQ=256):
    return pl.pallas_call(
        functools.partial(first_kernel, TQ),
        out_shape=(
            jax.ShapeDtypeStruct((NPTS, NPTS), f32),
            jax.ShapeDtypeStruct((2, NPTS, NPTS), f32),
        ),
        in_specs=[SM] + [VM] * 3,
        out_specs=(VM, VM),
        scratch_shapes=[pltpu.VMEM((4, NPTS, NORB), bf16)],
        compiler_params=pltpu.CompilerParams(vmem_limit_bytes=20 << 20),
        cost_estimate=pl.CostEstimate(flops=2_700_000_000, bytes_accessed=2 << 20, transcendentals=0),
    )(slots, x, g_mine, g_else)


def second_call(slots, x_own, x_next, g_mine, g_else, acc, own, core, TQ=256, TW=512):
    return pl.pallas_call(
        functools.partial(second_kernel, TQ, TW),
        out_shape=jax.ShapeDtypeStruct((2, NORB, NORB), bf16),
        in_specs=[SM] + [VM] * 7,
        out_specs=VM,
        scratch_shapes=[
            pltpu.VMEM((4, NPTS, NORB), bf16),
            pltpu.VMEM((NPTS, NPTS), bf16),
            pltpu.VMEM((NPTS, NPTS), bf16),
            pltpu.VMEM((2, NPTS, NORB), bf16),
        ],
        compiler_params=pltpu.CompilerParams(vmem_limit_bytes=32 << 20),
        cost_estimate=pl.CostEstimate(flops=8_300_000_000, bytes_accessed=4 << 20, transcendentals=0),
    )(slots, x_own, x_next, g_mine, g_else, acc, own, core)


def to_green(rows):
    parts = rows.reshape(64, 2, 2, 4, 128)
    return jnp.transpose(parts, (2, 0, 3, 1, 4)).reshape(2, NORB, NORB)


def local(green_freq, colloc, core):
    ta = lax.axis_index("ta")
    c = ta % 2
    pa = lax.axis_index("pa")
    xpos, ypos = pa // 16, (pa // 4) % 4
    cosine, sine = half_tables()
    table = jnp.where(ta < 2, cosine, sine)
    own_w = lax.dynamic_slice_in_dim(table, c * 64, 64, 1)
    other_w = lax.dynamic_slice_in_dim(table, 64 - c * 64, 64, 1)

    gf = green_freq.reshape(64, 2, 8, NORB)
    mine = lax.dynamic_index_in_dim(gf, c, 1, keepdims=False)
    theirs = lax.dynamic_index_in_dim(gf, 1 - c, 1, keepdims=False)
    arrived = lax.ppermute(theirs, "ta", CORE_SWAP)
    part = jnp.einsum("uw,wrj->urj", own_w, mine.astype(f32), precision=lax.Precision.HIGHEST)
    part += jnp.einsum("uw,wrj->urj", other_w, arrived.astype(f32), precision=lax.Precision.HIGHEST)
    part = part.astype(bf16).reshape(64, 8, 2, 128).swapaxes(1, 2).reshape(64, 16, 128)

    xt = jnp.swapaxes(colloc, 1, 2).reshape(2, 2, 16, 2, 128)
    xt = lax.dynamic_index_in_dim(xt, c, 0, keepdims=False).swapaxes(1, 2).reshape(4, 16, 128)
    xmsg = jnp.broadcast_to(xt.reshape(1, 2, 1, 2, 1, 16, 128), (2, 2, 2, 2, 4, 16, 128)).reshape(64, 16, 128)
    got = lax.all_to_all(jnp.concatenate([part, xmsg], 1), "pa", 0, 0, tiled=True)
    g_own = to_green(got[:, :16])
    xpart = got[:, 16:].reshape(NPTS, 128)

    g_kind = lax.ppermute(g_own, "ta", CHIP_SWAP)
    pieces = [xpart]
    for s in (1, 2, 3):
        pieces.append(lax.ppermute(xpart, ("ta", "pa"), square_pairs(s)))
    g_next = lax.ppermute(g_own, "ta", CORE_SWAP)
    x_own = jnp.stack(pieces)
    x_next = lax.ppermute(x_own, "ta", CORE_SWAP)
    g_last = lax.ppermute(g_kind, "ta", CORE_SWAP)
    here = 2 * (xpos % 2) + ypos % 2
    slots = jnp.arange(4, dtype=jnp.int32) ^ here
    acc, own = first_call(slots, x_own, g_own, g_kind)
    out = second_call(slots, x_own, x_next, g_next, g_last, acc, own, core)

    msg = out.reshape(2, 64, 4, NORB).swapaxes(0, 1).reshape(64, 8, NORB)
    back = lax.all_to_all(msg, "pa", 0, 0, tiled=True)
    back_next = lax.ppermute(back, "ta", CORE_SWAP)
    first = jnp.where(c == 0, back, back_next)
    second = jnp.where(c == 0, back_next, back)
    both = jnp.concatenate([first, second], 1)
    final = own_w * jnp.where(ta < 2, 2.0, -2.0)
    result = jnp.einsum("uw,urj->wrj", final, both.astype(f32), precision=lax.Precision.HIGHEST)
    return result.astype(bf16).reshape(64, 4, 4, NORB)


def solution(mesh):
    return jax.shard_map(
        local,
        mesh=mesh,
        in_specs=(P("ta", None, "pa", None), P(None, None, "pa"), P()),
        out_specs=P("ta", None, "pa", None),
        check_vma=False,
    )
```

time: 98.2 us -> 101 us (1.029)
  starting transfers between devices: 12.1 us -> 14.9 us
  Pallas kernels: 13.1 us -> 15.3 us
  blocking collectives: 51.3 us -> 49.7 us
    ppermute x6 -> x7, starting transfers between devices: 6.41 us -> 8.93 us  [the longest x3 5.16 us: local(): pieces.append(lax.ppermute(xpart, ('ta', 'pa'), square_pairs(s)))]
    pallas_call x1 -> x2, Pallas kernels: 13.1 us -> 15.3 us  [the longest x1 11.1 us: second_call(): pl.pallas_call(functools.partial(second_kernel, TQ, TW), out_shape=jax.Sh...]
    all_to_all x1, blocking collectives: 19.8 us -> 18.1 us  [local(): back = lax.all_to_all(msg, 'pa', 0, 0, tiled=True)]
    unnamed x4 -> x3, local copies, waits for them, and re-layouts: 1.39 us -> 0.07 us
    ppermute x6 -> x7, waiting for transfers between devices: 12.3 us -> 13.2 us  [the longest x1 6.66 us: local(): g_kind = lax.ppermute(g_own, 'ta', CHIP_SWAP)]
  transfers between devices with their start and end apart: 8 -> 9, of which waited for: 6 -> 5; matrix products, arithmetic and copies ran while one was open for 1% -> 2% of each run, Pallas kernels for 0% -> 4%
where the time goes in v2:
time: 101 us
  blocking collectives  49.7 us (49%)
  Pallas kernels  15.3 us (15%)
  starting transfers between devices  14.9 us (15%)
  waiting for transfers between devices  14.4 us (14%)
  local copies, waits for them, and re-layouts  4.46 us (4%)
  matrix products  1.54 us (2%)
    all_to_all x1, blocking collectives, local(): lax.all_to_all(jnp.concatenate([part, xmsg], 1), 'pa', 0, 0, tiled=True)  31.6 us
    all_to_all x1, blocking collectives, local(): back = lax.all_to_all(msg, 'pa', 0, 0, tiled=True)  18.1 us
    pallas_call x1, Pallas kernels, second_call(): pl.pallas_call(functools.partial(second_kernel, TQ, TW), out_shape=jax.Sh...  11.1 us
    ppermute x1, waiting for transfers between devices, local(): g_kind = lax.ppermute(g_own, 'ta', CHIP_SWAP)  6.66 us
    ppermute x3, waiting for transfers between devices, local(): pieces.append(lax.ppermute(xpart, ('ta', 'pa'), square_pairs(s)))  6.56 us
    ppermute x3, starting transfers between devices, local(): pieces.append(lax.ppermute(xpart, ('ta', 'pa'), square_pairs(s)))  5.16 us
    pallas_call x1, Pallas kernels, first_call(): pl.pallas_call(functools.partial(first_kernel, TQ), out_shape=(jax.ShapeD...  4.24 us
    ppermute x1, starting transfers between devices, local(): arrived = lax.ppermute(theirs, 'ta', CORE_SWAP)  3.29 us
  transfers between devices with their start and end apart: 9, of which 5 were waited for; matrix products, arithmetic and copies ran while one was open for 2% of the time, Pallas kernels for 4%

profile of v2, /device:TPU:1, one launch (start us, length us, event | category | flops | bytes accessed | tf_op | source)
XLA Modules:
  0.0 101.0 jit_solution(6614817721396680927)
XLA Ops:
  0.0 1.2 %copy.45 = bf16[64,4,4,256]{3,0,2,1:T(8,128)(2,1)S(1)} copy(bf16[64,4,4,256]{3,2,1,0:T(4,128)(2,1)} %param.3) | data formatting | bytes 1048576 | tf_op jit(solution)/shard_map/reshape | solution.py:167
  1.2 3.3 %collective-permute-start = (bf16[64,8,256]{2,0,1:T(8,128)(2,1)S(1)}, bf16[64,8,256]{2,0,1:T(8,128)(2,1)S(1)}, u32[]{:S(2)}, u32[]{:S(2)}) collective-permute-start(bf16[64,8,256]{2,0,1:T(8,128)(2,1)S(1)} %dynamic-slice_bitcast_fusion), channel_id=1, source_target_pairs={{0,64},{64,0},{128,192},{192,128},{1,65},{65,1},{129,193},{193,129... | collective-permute-start | bytes 786440 | tf_op jit(solution)/shard_map/ppermute | solution.py:170
  4.6 0.8 reshape.51
  5.4 0.2 multiply_select_fusion
  5.6 0.4 fusion.4
  6.0 0.4 fusion
  6.5 0.1 reshape.49
  6.5 0.3 copy.51
  6.9 31.6 %all_to_all.10 = bf16[64,32,128]{2,1,0:T(8,128)(2,1)S(1)} all-to-all(bf16[64,32,128]{2,1,0:T(8,128)(2,1)S(1)} %pad_maximum_fusion.1), channel_id=1, replica_groups=mesh['ta'=4,'pa'=64] {'pa'}, dimensions={0} | all-to-all | bytes 1048576 | tf_op jit(solution)/shard_map/all_to_all | solution.py:178
  38.6 0.5 collective-permute-start.1
  39.0 1.0 %collective-permute-start.2 = (bf16[1024,128]{1,0:T(8,128)(2,1)S(1)}, bf16[1024,128]{1,0:T(8,128)(2,1)S(1)}, u32[]{:S(2)}, u32[]{:S(2)}) collective-permute-start(bf16[1024,128]{1,0:T(8,128)(2,1)S(1)} %bitcast.48), channel_id=1, source_target_pairs={{0,16},{1,17},{2,18},{3,19},{4,20},{5,21},{6,22},{7,23},{8,24},{9,... | collective-permute-start | bytes 786440 | tf_op jit(solution)/shard_map/ppermute | solution.py:185
  40.1 3.6 %collective-permute-start.3 = (bf16[1024,128]{1,0:T(8,128)(2,1)S(1)}, bf16[1024,128]{1,0:T(8,128)(2,1)S(1)}, u32[]{:S(2)}, u32[]{:S(2)}) collective-permute-start(bf16[1024,128]{1,0:T(8,128)(2,1)S(1)} %bitcast.49), channel_id=1, source_target_pairs={{0,20},{1,21},{2,22},{3,23},{4,16},{5,17},{6,18},{7,19},{8,28},{9,... | collective-permute-start | bytes 786440 | tf_op jit(solution)/shard_map/ppermute | solution.py:185
  43.7 1.4 %collective-permute-done.1 = bf16[1024,128]{1,0:T(8,128)(2,1)S(1)} collective-permute-done((bf16[1024,128]{1,0:T(8,128)(2,1)S(1)}, bf16[1024,128]{1,0:T(8,128)(2,1)S(1)}, u32[]{:S(2)}, u32[]{:S(2)}) %collective-permute-start.1) | collective-permute-done | bytes 262176 | tf_op jit(solution)/shard_map/ppermute | solution.py:185
  45.1 0.4 collective-permute-done.2
  45.5 4.8 %collective-permute-done.3 = bf16[1024,128]{1,0:T(8,128)(2,1)S(1)} collective-permute-done((bf16[1024,128]{1,0:T(8,128)(2,1)S(1)}, bf16[1024,128]{1,0:T(8,128)(2,1)S(1)}, u32[]{:S(2)}, u32[]{:S(2)}) %collective-permute-start.3) | collective-permute-done | bytes 262176 | tf_op jit(solution)/shard_map/ppermute | solution.py:185
  50.3 0.1 pad_maximum_fusion.x_ref.x_own
  50.4 1.6 %collective-permute-start.4 = (bf16[4,1024,128]{2,1,0:T(8,128)(2,1)S(1)}, bf16[4,1024,128]{2,1,0:T(8,128)(2,1)S(1)}, u32[]{:S(2)}, u32[]{:S(2)}) collective-permute-start(bf16[4,1024,128]{2,1,0:T(8,128)(2,1)S(1)} %pad_maximum_fusion.x_ref.x_own), channel_id=1, source_target_pairs={{0,64},{64,0},{128,192},{192,128},{1,65},{65,1},{129,193},{193,129... | collective-permute-start | bytes 3145736 | tf_op jit(solution)/shard_map/ppermute | solution.py:188
  52.0 0.1 copy.46
  52.1 0.3 copy.36
  52.4 0.2 reshape.55.g_mine
  52.6 0.9 collective-permute-start.6
  53.5 0.4 collective-permute-start.5
  53.8 6.7 %collective-permute-done.6.g_else = bf16[2,256,256]{2,1,0:T(8,128)(2,1)S(1)} collective-permute-done((bf16[2,256,256]{2,1,0:T(8,128)(2,1)S(1)}, bf16[2,256,256]{2,1,0:T(8,128)(2,1)S(1)}, u32[]{:S(2)}, u32[]{:S(2)}) %collective-permute-start.6) | collective-permute-done | bytes 262176 | tf_op jit(solution)/shard_map/ppermute | solution.py:182
  60.5 0.9 collective-permute-start.7
  61.4 4.2 %shard_map.37 = (f32[1024,1024]{1,0:T(8,128)S(1)}, f32[2,1024,1024]{2,1,0:T(8,128)S(1)}) custom-call(s32[4]{0:T(128)S(1)} %iota_xor_fusion.slot_ref, bf16[4,1024,128]{2,1,0:T(8,128)(2,1)S(1)} %pad_maximum_fusion.x_ref.x_own, bf16[2,256,256]{2,1,0:T(8,128)(2,1)S(1)} %reshape.55.g_mine, bf16[2,256,256]{2,1,0:T(8,128)(2,1)S(1)} %collective-permute-done.6.g_else), custom_call_target="tpu_custom_call" | custom-call | flops 2700000000 | bytes 2097152 | tf_op jit(solution)/shard_map/pallas_call | solution.py:121
  65.7 11.1 %shard_map.38 = bf16[2,256,256]{2,1,0:T(8,128)(2,1)S(1)} custom-call(s32[4]{0:T(128)S(1)} %iota_xor_fusion.slot_ref, bf16[4,1024,128]{2,1,0:T(8,128)(2,1)S(1)} %pad_maximum_fusion.x_ref.x_own, bf16[4,1024,128]{2,1,0:T(8,128)(2,1)S(1)} %collective-permute-done.4.x_next, bf16[2,256,256]{2,1,0:T(8,128)(2,1)S(1)} %collective-permute-done.5.g_mine, ...), custom_call_target="tpu_custom_call" | custom-call | flops 8300000256 | bytes 4194304 | tf_op jit(solution)/shard_map/pallas_call | solution.py:136
  76.9 0.1 copy.37
  77.0 18.1 %all_to_all.11 = bf16[64,8,256]{2,1,0:T(8,128)(2,1)S(1)} all-to-all(bf16[64,8,256]{2,1,0:T(8,128)(2,1)S(1)} %reshape.57), channel_id=1, replica_groups=mesh['ta'=4,'pa'=64] {'pa'}, dimensions={0} | all-to-all | bytes 524288 | tf_op jit(solution)/shard_map/all_to_all | solution.py:196
  95.2 2.7 %collective-permute-start.8 = (bf16[64,8,256]{2,0,1:T(8,128)(2,1)S(1)}, bf16[64,8,256]{2,0,1:T(8,128)(2,1)S(1)}, u32[]{:S(2)}, u32[]{:S(2)}) collective-permute-start(bf16[64,8,256]{2,0,1:T(8,128)(2,1)S(1)} %copy.39), channel_id=1, source_target_pairs={{0,64},{64,0},{128,192},{192,128},{1,65},{65,1},{129,193},{193,129... | collective-permute-start | bytes 786440 | tf_op jit(solution)/shard_map/ppermute | solution.py:197
  97.9 1.2 %collective-permute-done.8 = bf16[64,8,256]{2,0,1:T(8,128)(2,1)S(1)} collective-permute-done((bf16[64,8,256]{2,0,1:T(8,128)(2,1)S(1)}, bf16[64,8,256]{2,0,1:T(8,128)(2,1)S(1)}, u32[]{:S(2)}, u32[]{:S(2)}) %collective-permute-start.8) | collective-permute-done | bytes 262176 | tf_op jit(solution)/shard_map/ppermute | solution.py:197
  99.1 0.7 convolution_convert_fusion
  99.8 1.2 %copy.42 = bf16[64,4,4,256]{3,2,1,0:T(4,128)(2,1)} copy(bf16[64,4,4,256]{3,0,2,1:T(8,128)(2,1)S(1)} %bitcast.39) | data formatting | bytes 1048576 | tf_op jit(solution)/shard_map/reshape | solution.py:203
  (19 shorter events, 0.4 us)
Async XLA Ops:
  1.2 4.8 %collective-permute-start = (bf16[64,8,256]{2,0,1:T(8,128)(2,1)S(1)}, bf16[64,8,256]{2,0,1:T(8,128)(2,1)S(1)}, u32[]{:S(2)}, u32[]{:S(2)}) collective-permute-start(bf16[64,8,256]{2,0,1:T(8,128)(2,1)S(1)} %dynamic-slice_bitcast_fusion), channel_id=1, source_target_pairs={{0,64},{64,0},{128,192},{192,128},{1,65},{65,1},{129,193},{193,129... | collective-permute-start | bytes 786440 | tf_op jit(solution)/shard_map/ppermute | solution.py:170
  38.6 6.5 %collective-permute-start.1 = (bf16[1024,128]{1,0:T(8,128)(2,1)S(1)}, bf16[1024,128]{1,0:T(8,128)(2,1)S(1)}, u32[]{:S(2)}, u32[]{:S(2)}) collective-permute-start(bf16[1024,128]{1,0:T(8,128)(2,1)S(1)} %bitcast.47), channel_id=1, source_target_pairs={{0,4},{1,5},{2,6},{3,7},{4,0},{5,1},{6,2},{7,3},{8,12},{9,13},{10,... | collective-permute-start | bytes 786440 | tf_op jit(solution)/shard_map/ppermute | solution.py:185
  39.0 6.4 %collective-permute-start.2 = (bf16[1024,128]{1,0:T(8,128)(2,1)S(1)}, bf16[1024,128]{1,0:T(8,128)(2,1)S(1)}, u32[]{:S(2)}, u32[]{:S(2)}) collective-permute-start(bf16[1024,128]{1,0:T(8,128)(2,1)S(1)} %bitcast.48), channel_id=1, source_target_pairs={{0,16},{1,17},{2,18},{3,19},{4,20},{5,21},{6,22},{7,23},{8,24},{9,... | collective-permute-start | bytes 786440 | tf_op jit(solution)/shard_map/ppermute | solution.py:185
  40.1 10.2 %collective-permute-start.3 = (bf16[1024,128]{1,0:T(8,128)(2,1)S(1)}, bf16[1024,128]{1,0:T(8,128)(2,1)S(1)}, u32[]{:S(2)}, u32[]{:S(2)}) collective-permute-start(bf16[1024,128]{1,0:T(8,128)(2,1)S(1)} %bitcast.49), channel_id=1, source_target_pairs={{0,20},{1,21},{2,22},{3,23},{4,16},{5,17},{6,18},{7,19},{8,28},{9,... | collective-permute-start | bytes 786440 | tf_op jit(solution)/shard_map/ppermute | solution.py:185
  50.4 15.2 %collective-permute-start.4 = (bf16[4,1024,128]{2,1,0:T(8,128)(2,1)S(1)}, bf16[4,1024,128]{2,1,0:T(8,128)(2,1)S(1)}, u32[]{:S(2)}, u32[]{:S(2)}) collective-permute-start(bf16[4,1024,128]{2,1,0:T(8,128)(2,1)S(1)} %pad_maximum_fusion.x_ref.x_own), channel_id=1, source_target_pairs={{0,64},{64,0},{128,192},{192,128},{1,65},{65,1},{129,193},{193,129... | collective-permute-start | bytes 3145736 | tf_op jit(solution)/shard_map/ppermute | solution.py:188
  52.6 7.9 %collective-permute-start.6 = (bf16[2,256,256]{2,1,0:T(8,128)(2,1)S(1)}, bf16[2,256,256]{2,1,0:T(8,128)(2,1)S(1)}, u32[]{:S(2)}, u32[]{:S(2)}) collective-permute-start(bf16[2,256,256]{2,1,0:T(8,128)(2,1)S(1)} %reshape.55.g_mine), channel_id=1, source_target_pairs={{0,128},{128,0},{64,192},{192,64},{1,129},{129,1},{65,193},{193,65... | collective-permute-start | bytes 786440 | tf_op jit(solution)/shard_map/ppermute | solution.py:182
  53.5 12.2 %collective-permute-start.5 = (bf16[2,256,256]{2,1,0:T(8,128)(2,1)S(1)}, bf16[2,256,256]{2,1,0:T(8,128)(2,1)S(1)}, u32[]{:S(2)}, u32[]{:S(2)}) collective-permute-start(bf16[2,256,256]{2,1,0:T(8,128)(2,1)S(1)} %reshape.55.g_mine), channel_id=1, source_target_pairs={{0,64},{64,0},{128,192},{192,128},{1,65},{65,1},{129,193},{193,129... | collective-permute-start | bytes 786440 | tf_op jit(solution)/shard_map/ppermute | solution.py:186
  60.5 5.1 %collective-permute-start.7 = (bf16[2,256,256]{2,1,0:T(8,128)(2,1)S(1)}, bf16[2,256,256]{2,1,0:T(8,128)(2,1)S(1)}, u32[]{:S(2)}, u32[]{:S(2)}) collective-permute-start(bf16[2,256,256]{2,1,0:T(8,128)(2,1)S(1)} %collective-permute-done.6.g_else), channel_id=1, source_target_pairs={{0,64},{64,0},{128,192},{192,128},{1,65},{65,1},{129,193},{193,129... | collective-permute-start | bytes 786440 | tf_op jit(solution)/shard_map/ppermute | solution.py:189
  61.4 4.3 %copy-start = (bf16[1024,1024]{1,0:T(8,128)(2,1)S(1)}, bf16[1024,1024]{1,0:T(8,128)(2,1)}, u32[]{:S(2)}) copy-start(bf16[1024,1024]{1,0:T(8,128)(2,1)} %core_ref.1) | copy-start | bytes 6291460
  95.2 3.8 %collective-permute-start.8 = (bf16[64,8,256]{2,0,1:T(8,128)(2,1)S(1)}, bf16[64,8,256]{2,0,1:T(8,128)(2,1)S(1)}, u32[]{:S(2)}, u32[]{:S(2)}) collective-permute-start(bf16[64,8,256]{2,0,1:T(8,128)(2,1)S(1)} %copy.39), channel_id=1, source_target_pairs={{0,64},{64,0},{128,192},{192,128},{1,65},{65,1},{129,193},{193,129... | collective-permute-start | bytes 786440 | tf_op jit(solution)/shard_map/ppermute | solution.py:197

commit v3 on v2

v3 whole, which is shorter than its diff:
```python
import functools

import jax
import jax.numpy as jnp
from jax import lax
from jax.experimental import pallas as pl
from jax.experimental.pallas import tpu as pltpu
from jax.sharding import PartitionSpec as P


NFREQ = 128
NPTS = 1024
NORB = 256
bf16 = jnp.bfloat16
f32 = jnp.float32

CORE_SWAP = [(0, 1), (1, 0), (2, 3), (3, 2)]
CHIP_SWAP = [(0, 2), (2, 0), (1, 3), (3, 1)]
NT = ((1,), (1,))
TN = ((0,), (0,))


def square_pairs(step):
    def partner(v, core):
        return v ^ 1 if core == 0 else ((v + 1) ^ 1) - 1 & 3

    pairs = []
    for ta in range(4):
        for i in range(64):
            x, y, z = i // 16, (i // 4) % 4, i % 4
            x = partner(x, ta % 2) if step & 2 else x
            y = partner(y, ta % 2) if step & 1 else y
            pairs.append((ta * 64 + i, ta * 64 + x * 16 + y * 4 + z))
    return pairs


def half_tables():
    freq = jnp.arange(NFREQ, dtype=f32)
    times = jnp.arange(NFREQ // 2, dtype=f32)
    phase = jnp.pi * (2.0 * freq[None, :] + 1.0) * (times[:, None] + 0.5) / NFREQ
    scale = 1.0 / jnp.sqrt(f32(NFREQ))
    return jnp.cos(phase) * scale, jnp.sin(phase) * scale


def dot(a, b, dims=((1,), (0,))):
    return lax.dot_general(a, b, (dims, ((), ())), preferred_element_type=f32)


HALF = NPTS // 2


def square_place():
    pa = lax.axis_index("pa")
    return 2 * ((pa // 16) % 2) + (pa // 4) % 2


def points_of(x_ref, here, kk, rows):
    return jnp.concatenate([x_ref[(2 * kk) ^ here, rows, :], x_ref[(2 * kk + 1) ^ here, rows, :]], axis=1)


def term_columns(half, x_ref, t_ref, own_ref, term_ref):
    here = square_place()
    acc = None
    for kk in range(2):
        xq = points_of(x_ref, here, kk, pl.ds(half * HALF, HALF))
        v = dot(t_ref[kk], xq, NT)
        own_ref[kk] = v
        w = dot(t_ref[2 + kk], xq, NT)
        acc = v * v - w * w if acc is None else acc + (v * v - w * w)
    term_ref[...] = acc.astype(bf16)


def first_kernel(x_ref, g_mine, g_else, t_ref, own_ref, term_ref):
    here = square_place()
    for kk in range(2):
        xk = points_of(x_ref, here, kk, pl.ds(0, NPTS))
        t_ref[kk] = dot(xk, g_mine[kk]).astype(bf16)
        t_ref[2 + kk] = dot(xk, g_else[kk]).astype(bf16)
    term_columns(0, x_ref, t_ref, own_ref, term_ref)


def second_kernel(x_ref, t_ref, own_ref, term_ref):
    term_columns(1, x_ref, t_ref, own_ref, term_ref)


def bubble_of(term0, term1):
    return ((term0[...].astype(f32) + term1[...].astype(f32)) * 0.25).astype(bf16)


def third_kernel(TW, core_ref, term0, term1, mix_ref, bub_ref):
    bub_ref[...] = bubble_of(term0, term1)

    def step(i, _):
        rows = pl.ds(pl.multiple_of(i * TW, TW), TW)
        mix_ref[rows, :] = dot(core_ref[rows, :], bub_ref[...]).astype(bf16)
        return 0

    lax.fori_loop(0, NPTS // TW, step, 0)


def fourth_kernel(TW, core_ref, mix0, term0, term1, own0, own1, x_ref, out_ref, bub_ref, mix1, tmp_ref):
    here = square_place()
    every = pl.ds(0, NPTS)
    third_kernel(TW, core_ref, term0, term1, mix1, bub_ref)

    def step(i, _):
        rows = pl.ds(pl.multiple_of(i * TW, TW), TW)
        w = dot(jnp.concatenate([mix0[rows, :], mix1[rows, :]], axis=1), core_ref[...])
        for kk in range(2):
            own = jnp.concatenate([own0[kk, rows, :], own1[kk, rows, :]], axis=1)
            source = (own * w).astype(bf16)
            tmp_ref[kk, rows, :] = dot(source, points_of(x_ref, here, kk, every)).astype(bf16)
        return 0

    lax.fori_loop(0, NPTS // TW, step, 0)
    for kk in range(2):
        out_ref[kk] = dot(points_of(x_ref, here, kk, every), tmp_ref[kk], TN).astype(bf16)


VM = pl.BlockSpec(memory_space=pltpu.VMEM)


def call(kernel, n_in, outs, scratch, gflops, limit):
    return pl.pallas_call(
        kernel,
        out_shape=tuple(jax.ShapeDtypeStruct(*o) for o in outs),
        in_specs=[VM] * n_in,
        out_specs=tuple(VM for _ in outs),
        scratch_shapes=[pltpu.VMEM(*o) for o in scratch],
        compiler_params=pltpu.CompilerParams(vmem_limit_bytes=limit << 20),
        cost_estimate=pl.CostEstimate(flops=int(gflops * 1e9), bytes_accessed=2 << 20, transcendentals=0),
    )


T_OUT = ((4, NPTS, NORB), bf16)
OWN_OUT = ((2, NPTS, HALF), f32)
HALF_OUT = ((NPTS, HALF), bf16)


def to_green(rows):
    parts = rows.reshape(64, 2, 2, 4, 128)
    return jnp.transpose(parts, (2, 0, 3, 1, 4)).reshape(2, NORB, NORB)


def local(green_freq, colloc, core):
    ta = lax.axis_index("ta")
    c = ta % 2
    cosine, sine = half_tables()
    table = jnp.where(ta < 2, cosine, sine)
    own_w = lax.dynamic_slice_in_dim(table, c * 64, 64, 1)
    other_w = lax.dynamic_slice_in_dim(table, 64 - c * 64, 64, 1)

    gf = green_freq.reshape(64, 2, 8, NORB)
    mine = lax.dynamic_index_in_dim(gf, c, 1, keepdims=False)
    theirs = lax.dynamic_index_in_dim(gf, 1 - c, 1, keepdims=False)
    arrived = lax.ppermute(theirs, "ta", CORE_SWAP)
    part = jnp.einsum("uw,wrj->urj", own_w, mine.astype(f32), precision=lax.Precision.HIGHEST)
    part += jnp.einsum("uw,wrj->urj", other_w, arrived.astype(f32), precision=lax.Precision.HIGHEST)
    part = part.astype(bf16).reshape(64, 8, 2, 128).swapaxes(1, 2).reshape(64, 16, 128)

    xt = jnp.swapaxes(colloc, 1, 2).reshape(2, 2, 16, 2, 128)
    xt = lax.dynamic_index_in_dim(xt, c, 0, keepdims=False).swapaxes(1, 2).reshape(4, 16, 128)
    xmsg = jnp.broadcast_to(xt.reshape(1, 2, 1, 2, 1, 16, 128), (2, 2, 2, 2, 4, 16, 128)).reshape(64, 16, 128)
    got = lax.all_to_all(jnp.concatenate([part, xmsg], 1), "pa", 0, 0, tiled=True)
    g_own = to_green(got[:, :16])
    xpart = got[:, 16:].reshape(NPTS, 128)

    g_kind = lax.ppermute(g_own, "ta", CHIP_SWAP)
    pieces = [xpart]
    for s in (1, 2, 3):
        pieces.append(lax.ppermute(xpart, ("ta", "pa"), square_pairs(s)))
    x_own = jnp.stack(pieces)
    t, own0, term0 = call(first_kernel, 3, (T_OUT, OWN_OUT, HALF_OUT), (), 1.6, 16)(x_own, g_own, g_kind)
    term0_next = lax.ppermute(term0, "ta", CORE_SWAP)
    own1, term1 = call(second_kernel, 2, (OWN_OUT, HALF_OUT), (), 1.1, 16)(x_own, t)
    term1_next = lax.ppermute(term1, "ta", CORE_SWAP)
    (mix0,) = call(functools.partial(third_kernel, 512), 3, (HALF_OUT,), (HALF_OUT,), 1.1, 8)(core, term0, term0_next)
    (out,) = call(
        functools.partial(fourth_kernel, 512),
        7,
        (((2, NORB, NORB), bf16),),
        (HALF_OUT, HALF_OUT, ((2, NPTS, NORB), bf16)),
        4.6,
        20,
    )(core, mix0, term1, term1_next, own0, own1, x_own)

    msg = out.reshape(2, 64, 4, NORB).swapaxes(0, 1).reshape(64, 8, NORB)
    back = lax.all_to_all(msg, "pa", 0, 0, tiled=True)
    back_next = lax.ppermute(back, "ta", CORE_SWAP)
    first = jnp.where(c == 0, back, back_next)
    second = jnp.where(c == 0, back_next, back)
    both = jnp.concatenate([first, second], 1)
    final = own_w * jnp.where(ta < 2, 2.0, -2.0)
    result = jnp.einsum("uw,urj->wrj", final, both.astype(f32), precision=lax.Precision.HIGHEST)
    return result.astype(bf16).reshape(64, 4, 4, NORB)


def solution(mesh):
    return jax.shard_map(
        local,
        mesh=mesh,
        in_specs=(P("ta", None, "pa", None), P(None, None, "pa"), P()),
        out_specs=P("ta", None, "pa", None),
        check_vma=False,
    )
```

time: 101 us -> 90.1 us (0.89)
  waiting for transfers between devices: 14.4 us -> 7.78 us
  Pallas kernels: 15.3 us -> 11 us
    ppermute x1, waiting for transfers between devices: 6.66 us -> 1.83 us  [local(): g_kind = lax.ppermute(g_own, 'ta', CHIP_SWAP)]
    pallas_call x2 -> x4, Pallas kernels: 15.3 us -> 11 us  [the longest x1 5.87 us: local(): call(functools.partial(fourth_kernel, 512), 7, (((2, NORB, NORB), bf16),)...]
    ppermute x3, waiting for transfers between devices: 6.56 us -> 3.88 us  [local(): pieces.append(lax.ppermute(xpart, ('ta', 'pa'), square_pairs(s)))]
    ppermute x1, starting transfers between devices: 0.89 us -> 2.01 us  [local(): g_kind = lax.ppermute(g_own, 'ta', CHIP_SWAP)]
    ppermute x3 -> x2, starting transfers between devices: 2.88 us -> 1.79 us  [the longest x1 1.49 us: local(): term0_next = lax.ppermute(term0, 'ta', CORE_SWAP)]
  transfers between devices with their start and end apart: 9 -> 8, of which waited for: 5 -> 7; matrix products, arithmetic and copies ran while one was open for 2% -> 2% of each run, Pallas kernels for 4% -> 4%
where the time goes in v3:
time: 90.1 us; the launch traced here: 89.9 us
  blocking collectives  49.2 us (55%)
  starting transfers between devices  15.4 us (17%)
  Pallas kernels  11 us (12%)
  waiting for transfers between devices  7.78 us (9%)
  local copies, waits for them, and re-layouts  4.33 us (5%)
  matrix products  1.55 us (2%)
    all_to_all x1, blocking collectives, local(): lax.all_to_all(jnp.concatenate([part, xmsg], 1), 'pa', 0, 0, tiled=True)  31.6 us
    all_to_all x1, blocking collectives, local(): back = lax.all_to_all(msg, 'pa', 0, 0, tiled=True)  17.5 us
    pallas_call x1, Pallas kernels, local(): call(functools.partial(fourth_kernel, 512), 7, (((2, NORB, NORB), bf16),)...  5.87 us
    ppermute x3, starting transfers between devices, local(): pieces.append(lax.ppermute(xpart, ('ta', 'pa'), square_pairs(s)))  5.16 us
    ppermute x3, waiting for transfers between devices, local(): pieces.append(lax.ppermute(xpart, ('ta', 'pa'), square_pairs(s)))  3.88 us
    ppermute x1, starting transfers between devices, local(): arrived = lax.ppermute(theirs, 'ta', CORE_SWAP)  3.29 us
    ppermute x1, starting transfers between devices, local(): back_next = lax.ppermute(back, 'ta', CORE_SWAP)  3.19 us
    ppermute x1, starting transfers between devices, local(): g_kind = lax.ppermute(g_own, 'ta', CHIP_SWAP)  2.01 us
  transfers between devices with their start and end apart: 8, of which 7 were waited for; matrix products, arithmetic and copies ran while one was open for 2% of the time, Pallas kernels for 4%

profile of v3, /device:TPU:1, one launch (start us, length us, event | category | flops | bytes accessed | tf_op | source)
XLA Modules:
  0.0 89.9 jit_solution(13833860252786795756)
XLA Ops:
  0.0 1.2 %copy.39 = bf16[64,4,4,256]{3,0,2,1:T(8,128)(2,1)S(1)} copy(bf16[64,4,4,256]{3,2,1,0:T(4,128)(2,1)} %param.3) | data formatting | bytes 1048576 | tf_op jit(solution)/shard_map/reshape | solution.py:153
  1.2 3.3 %collective-permute-start = (bf16[64,8,256]{2,0,1:T(8,128)(2,1)S(1)}, bf16[64,8,256]{2,0,1:T(8,128)(2,1)S(1)}, u32[]{:S(2)}, u32[]{:S(2)}) collective-permute-start(bf16[64,8,256]{2,0,1:T(8,128)(2,1)S(1)} %dynamic-slice_bitcast_fusion), channel_id=1, source_target_pairs={{0,64},{64,0},{128,192},{192,128},{1,65},{65,1},{129,193},{193,129... | collective-permute-start | bytes 786440 | tf_op jit(solution)/shard_map/ppermute | solution.py:156
  4.5 0.8 reshape.51
  5.4 0.2 multiply_select_fusion
  5.6 0.4 fusion.4
  6.0 0.4 fusion
  6.5 0.3 copy.46
  6.9 31.6 %all_to_all.10 = bf16[64,32,128]{2,1,0:T(8,128)(2,1)S(1)} all-to-all(bf16[64,32,128]{2,1,0:T(8,128)(2,1)S(1)} %pad_maximum_fusion.1), channel_id=1, replica_groups=mesh['ta'=4,'pa'=64] {'pa'}, dimensions={0} | all-to-all | bytes 1048576 | tf_op jit(solution)/shard_map/all_to_all | solution.py:164
  38.6 1.2 %collective-permute-start.3 = (bf16[1024,128]{1,0:T(8,128)(2,1)S(1)}, bf16[1024,128]{1,0:T(8,128)(2,1)S(1)}, u32[]{:S(2)}, u32[]{:S(2)}) collective-permute-start(bf16[1024,128]{1,0:T(8,128)(2,1)S(1)} %bitcast.49), channel_id=1, source_target_pairs={{0,20},{1,21},{2,22},{3,23},{4,16},{5,17},{6,18},{7,19},{8,28},{9,... | collective-permute-start | bytes 786440 | tf_op jit(solution)/shard_map/ppermute | solution.py:171
  39.8 1.7 %collective-permute-start.2 = (bf16[1024,128]{1,0:T(8,128)(2,1)S(1)}, bf16[1024,128]{1,0:T(8,128)(2,1)S(1)}, u32[]{:S(2)}, u32[]{:S(2)}) collective-permute-start(bf16[1024,128]{1,0:T(8,128)(2,1)S(1)} %bitcast.50), channel_id=1, source_target_pairs={{0,16},{1,17},{2,18},{3,19},{4,20},{5,21},{6,22},{7,23},{8,24},{9,... | collective-permute-start | bytes 786440 | tf_op jit(solution)/shard_map/ppermute | solution.py:171
  41.5 2.3 %collective-permute-start.1 = (bf16[1024,128]{1,0:T(8,128)(2,1)S(1)}, bf16[1024,128]{1,0:T(8,128)(2,1)S(1)}, u32[]{:S(2)}, u32[]{:S(2)}) collective-permute-start(bf16[1024,128]{1,0:T(8,128)(2,1)S(1)} %bitcast.51), channel_id=1, source_target_pairs={{0,4},{1,5},{2,6},{3,7},{4,0},{5,1},{6,2},{7,3},{8,12},{9,13},{10,... | collective-permute-start | bytes 786440 | tf_op jit(solution)/shard_map/ppermute | solution.py:171
  43.8 0.2 copy.45
  44.0 0.2 reshape.55.g_mine
  44.1 2.0 %collective-permute-start.4 = (bf16[2,256,256]{2,1,0:T(8,128)(2,1)S(1)}, bf16[2,256,256]{2,1,0:T(8,128)(2,1)S(1)}, u32[]{:S(2)}, u32[]{:S(2)}) collective-permute-start(bf16[2,256,256]{2,1,0:T(8,128)(2,1)S(1)} %reshape.55.g_mine), channel_id=1, source_target_pairs={{0,128},{128,0},{64,192},{192,64},{1,129},{129,1},{65,193},{193,65... | collective-permute-start | bytes 786440 | tf_op jit(solution)/shard_map/ppermute | solution.py:168
  46.2 1.2 %collective-permute-done.3 = bf16[1024,128]{1,0:T(8,128)(2,1)S(1)} collective-permute-done((bf16[1024,128]{1,0:T(8,128)(2,1)S(1)}, bf16[1024,128]{1,0:T(8,128)(2,1)S(1)}, u32[]{:S(2)}, u32[]{:S(2)}) %collective-permute-start.3) | collective-permute-done | bytes 262176 | tf_op jit(solution)/shard_map/ppermute | solution.py:171
  47.3 0.9 collective-permute-done.2
  48.2 1.9 %collective-permute-done.1 = bf16[1024,128]{1,0:T(8,128)(2,1)S(1)} collective-permute-done((bf16[1024,128]{1,0:T(8,128)(2,1)S(1)}, bf16[1024,128]{1,0:T(8,128)(2,1)S(1)}, u32[]{:S(2)}, u32[]{:S(2)}) %collective-permute-start.1) | collective-permute-done | bytes 262176 | tf_op jit(solution)/shard_map/ppermute | solution.py:171
  50.0 0.1 pad_maximum_fusion.x_ref
  50.2 1.8 %collective-permute-done.4.g_else = bf16[2,256,256]{2,1,0:T(8,128)(2,1)S(1)} collective-permute-done((bf16[2,256,256]{2,1,0:T(8,128)(2,1)S(1)}, bf16[2,256,256]{2,1,0:T(8,128)(2,1)S(1)}, u32[]{:S(2)}, u32[]{:S(2)}) %collective-permute-start.4) | collective-permute-done | bytes 262176 | tf_op jit(solution)/shard_map/ppermute | solution.py:168
  52.0 2.0 %shard_map.37 = (bf16[4,1024,256]{2,1,0:T(8,128)(2,1)S(1)}, f32[2,1024,512]{2,1,0:T(8,128)S(1)}, bf16[1024,512]{1,0:T(8,128)(2,1)S(1)}) custom-call(bf16[4,1024,128]{2,1,0:T(8,128)(2,1)S(1)} %pad_maximum_fusion.x_ref, bf16[2,256,256]{2,1,0:T(8,128)(2,1)S(1)} %reshape.55.g_mine, bf16[2,256,256]{2,1,0:T(8,128)(2,1)S(1)} %collective-permute-done.4.g_else), custom_call_target="tpu_custom_call" | custom-call | flops 1600000000 | bytes 2097152 | tf_op jit(solution)/shard_map/pallas_call | solution.py:173
  54.0 1.5 %collective-permute-start.5 = (bf16[1024,512]{1,0:T(8,128)(2,1)S(1)}, bf16[1024,512]{1,0:T(8,128)(2,1)S(1)}, u32[]{:S(2)}, u32[]{:S(2)}) collective-permute-start(bf16[1024,512]{1,0:T(8,128)(2,1)S(1)} %get-tuple-element.10.term0), channel_id=1, source_target_pairs={{0,64},{64,0},{128,192},{192,128},{1,65},{65,1},{129,193},{193,129... | collective-permute-start | bytes 3145736 | tf_op jit(solution)/shard_map/ppermute | solution.py:174
  55.5 1.4 %shard_map.39 = (f32[2,1024,512]{2,1,0:T(8,128)S(1)}, bf16[1024,512]{1,0:T(8,128)(2,1)S(1)}) custom-call(bf16[4,1024,128]{2,1,0:T(8,128)(2,1)S(1)} %pad_maximum_fusion.x_ref, bf16[4,1024,256]{2,1,0:T(8,128)(2,1)S(1)} %get-tuple-element.11.t_ref), custom_call_target="tpu_custom_call" | custom-call | flops 1100000000 | bytes 2097152 | tf_op jit(solution)/shard_map/pallas_call | solution.py:175
  56.9 0.3 collective-permute-start.6
  57.2 0.5 collective-permute-done.5.term1
  57.8 1.7 %shard_map.38.mix0 = bf16[1024,512]{1,0:T(8,128)(2,1)S(1)} custom-call(bf16[1024,1024]{1,0:T(8,128)(2,1)S(1)} %copy-done, bf16[1024,512]{1,0:T(8,128)(2,1)S(1)} %get-tuple-element.10.term0, bf16[1024,512]{1,0:T(8,128)(2,1)S(1)} %collective-permute-done.5.term1), custom_call_target="tpu_custom_call" | custom-call | flops 1100000000 | bytes 2097152 | tf_op jit(solution)/shard_map/pallas_call | solution.py:177
  59.5 0.4 collective-permute-done.6.term1
  59.9 5.9 %shard_map.40 = bf16[2,256,256]{2,1,0:T(8,128)(2,1)S(1)} custom-call(bf16[1024,1024]{1,0:T(8,128)(2,1)S(1)} %copy-done, bf16[1024,512]{1,0:T(8,128)(2,1)S(1)} %shard_map.38.mix0, bf16[1024,512]{1,0:T(8,128)(2,1)S(1)} %get-tuple-element.12.term0, bf16[1024,512]{1,0:T(8,128)(2,1)S(1)} %collective-permute-done.6.term1, ...), custom_call_target="tpu_custom_call" | custom-call | flops 4600000000 | bytes 2097152 | tf_op jit(solution)/shard_map/pallas_call | solution.py:178
  66.0 17.5 %all_to_all.11 = bf16[64,8,256]{2,1,0:T(8,128)(2,1)S(1)} all-to-all(bf16[64,8,256]{2,1,0:T(8,128)(2,1)S(1)} %reshape.57), channel_id=1, replica_groups=mesh['ta'=4,'pa'=64] {'pa'}, dimensions={0} | all-to-all | bytes 524288 | tf_op jit(solution)/shard_map/all_to_all | solution.py:188
  83.6 3.2 %collective-permute-start.7 = (bf16[64,8,256]{2,0,1:T(8,128)(2,1)S(1)}, bf16[64,8,256]{2,0,1:T(8,128)(2,1)S(1)}, u32[]{:S(2)}, u32[]{:S(2)}) collective-permute-start(bf16[64,8,256]{2,0,1:T(8,128)(2,1)S(1)} %copy.33), channel_id=1, source_target_pairs={{0,64},{64,0},{128,192},{192,128},{1,65},{65,1},{129,193},{193,129... | collective-permute-start | bytes 786440 | tf_op jit(solution)/shard_map/ppermute | solution.py:189
  86.7 1.2 %collective-permute-done.7 = bf16[64,8,256]{2,0,1:T(8,128)(2,1)S(1)} collective-permute-done((bf16[64,8,256]{2,0,1:T(8,128)(2,1)S(1)}, bf16[64,8,256]{2,0,1:T(8,128)(2,1)S(1)}, u32[]{:S(2)}, u32[]{:S(2)}) %collective-permute-start.7) | collective-permute-done | bytes 262176 | tf_op jit(solution)/shard_map/ppermute | solution.py:189
  88.0 0.7 convolution_convert_fusion
  88.7 1.2 %copy.36 = bf16[64,4,4,256]{3,2,1,0:T(4,128)(2,1)} copy(bf16[64,4,4,256]{3,0,2,1:T(8,128)(2,1)S(1)} %bitcast.40) | data formatting | bytes 1048576 | tf_op jit(solution)/shard_map/reshape | solution.py:195
  (17 shorter events, 0.6 us)
Async XLA Ops:
  1.2 4.8 %collective-permute-start = (bf16[64,8,256]{2,0,1:T(8,128)(2,1)S(1)}, bf16[64,8,256]{2,0,1:T(8,128)(2,1)S(1)}, u32[]{:S(2)}, u32[]{:S(2)}) collective-permute-start(bf16[64,8,256]{2,0,1:T(8,128)(2,1)S(1)} %dynamic-slice_bitcast_fusion), channel_id=1, source_target_pairs={{0,64},{64,0},{128,192},{192,128},{1,65},{65,1},{129,193},{193,129... | collective-permute-start | bytes 786440 | tf_op jit(solution)/shard_map/ppermute | solution.py:156
  38.6 8.7 %collective-permute-start.3 = (bf16[1024,128]{1,0:T(8,128)(2,1)S(1)}, bf16[1024,128]{1,0:T(8,128)(2,1)S(1)}, u32[]{:S(2)}, u32[]{:S(2)}) collective-permute-start(bf16[1024,128]{1,0:T(8,128)(2,1)S(1)} %bitcast.49), channel_id=1, source_target_pairs={{0,20},{1,21},{2,22},{3,23},{4,16},{5,17},{6,18},{7,19},{8,28},{9,... | collective-permute-start | bytes 786440 | tf_op jit(solution)/shard_map/ppermute | solution.py:171
  39.8 8.4 %collective-permute-start.2 = (bf16[1024,128]{1,0:T(8,128)(2,1)S(1)}, bf16[1024,128]{1,0:T(8,128)(2,1)S(1)}, u32[]{:S(2)}, u32[]{:S(2)}) collective-permute-start(bf16[1024,128]{1,0:T(8,128)(2,1)S(1)} %bitcast.50), channel_id=1, source_target_pairs={{0,16},{1,17},{2,18},{3,19},{4,20},{5,21},{6,22},{7,23},{8,24},{9,... | collective-permute-start | bytes 786440 | tf_op jit(solution)/shard_map/ppermute | solution.py:171
  41.5 8.6 %collective-permute-start.1 = (bf16[1024,128]{1,0:T(8,128)(2,1)S(1)}, bf16[1024,128]{1,0:T(8,128)(2,1)S(1)}, u32[]{:S(2)}, u32[]{:S(2)}) collective-permute-start(bf16[1024,128]{1,0:T(8,128)(2,1)S(1)} %bitcast.51), channel_id=1, source_target_pairs={{0,4},{1,5},{2,6},{3,7},{4,0},{5,1},{6,2},{7,3},{8,12},{9,13},{10,... | collective-permute-start | bytes 786440 | tf_op jit(solution)/shard_map/ppermute | solution.py:171
  44.1 7.9 %collective-permute-start.4 = (bf16[2,256,256]{2,1,0:T(8,128)(2,1)S(1)}, bf16[2,256,256]{2,1,0:T(8,128)(2,1)S(1)}, u32[]{:S(2)}, u32[]{:S(2)}) collective-permute-start(bf16[2,256,256]{2,1,0:T(8,128)(2,1)S(1)} %reshape.55.g_mine), channel_id=1, source_target_pairs={{0,128},{128,0},{64,192},{192,64},{1,129},{129,1},{65,193},{193,65... | collective-permute-start | bytes 786440 | tf_op jit(solution)/shard_map/ppermute | solution.py:168
  50.2 7.6 %copy-start = (bf16[1024,1024]{1,0:T(8,128)(2,1)S(1)}, bf16[1024,1024]{1,0:T(8,128)(2,1)}, u32[]{:S(2)}) copy-start(bf16[1024,1024]{1,0:T(8,128)(2,1)} %core_ref.3) | copy-start | bytes 6291460
  54.0 3.8 %collective-permute-start.5 = (bf16[1024,512]{1,0:T(8,128)(2,1)S(1)}, bf16[1024,512]{1,0:T(8,128)(2,1)S(1)}, u32[]{:S(2)}, u32[]{:S(2)}) collective-permute-start(bf16[1024,512]{1,0:T(8,128)(2,1)S(1)} %get-tuple-element.10.term0), channel_id=1, source_target_pairs={{0,64},{64,0},{128,192},{192,128},{1,65},{65,1},{129,193},{193,129... | collective-permute-start | bytes 3145736 | tf_op jit(solution)/shard_map/ppermute | solution.py:174
  56.9 2.9 %collective-permute-start.6 = (bf16[1024,512]{1,0:T(8,128)(2,1)S(1)}, bf16[1024,512]{1,0:T(8,128)(2,1)S(1)}, u32[]{:S(2)}, u32[]{:S(2)}) collective-permute-start(bf16[1024,512]{1,0:T(8,128)(2,1)S(1)} %get-tuple-element.12.term0), channel_id=1, source_target_pairs={{0,64},{64,0},{128,192},{192,128},{1,65},{65,1},{129,193},{193,129... | collective-permute-start | bytes 3145736 | tf_op jit(solution)/shard_map/ppermute | solution.py:176
  83.6 4.3 %collective-permute-start.7 = (bf16[64,8,256]{2,0,1:T(8,128)(2,1)S(1)}, bf16[64,8,256]{2,0,1:T(8,128)(2,1)S(1)}, u32[]{:S(2)}, u32[]{:S(2)}) collective-permute-start(bf16[64,8,256]{2,0,1:T(8,128)(2,1)S(1)} %copy.33), channel_id=1, source_target_pairs={{0,64},{64,0},{128,192},{192,128},{1,65},{65,1},{129,193},{193,129... | collective-permute-start | bytes 786440 | tf_op jit(solution)/shard_map/ppermute | solution.py:189

commit v4 on v3

--- a/solution.py
+++ b/solution.py
@@ -115,6 +115,66 @@
     lax.fori_loop(0, NPTS // TW, step, 0)
     for kk in range(2):
         out_ref[kk] = dot(points_of(x_ref, here, kk, every), tmp_ref[kk], TN).astype(bf16)
+
+
+def split(x):
+    high = x.astype(bf16)
+    return high, (x - high.astype(f32)).astype(bf16)
+
+
+def one_hot(shape, which):
+    r = lax.broadcasted_iota(jnp.int32, shape, 0)
+    c = lax.broadcasted_iota(jnp.int32, shape, 1)
+    return ((r >> 3) == c if which == 0 else r == (c >> 3)).astype(f32).astype(bf16)
+
+
+def spread(table, dims):
+    r = lax.broadcasted_iota(jnp.int32, (512, 512), 0)
+    c = lax.broadcasted_iota(jnp.int32, (512, 512), 1)
+    wide = dot(one_hot((512, 64), 0), table, dims).astype(bf16)
+    return jnp.where(((r ^ c) & 7) == 0, dot(wide, one_hot((64, 512), 1)), 0.0).astype(bf16)
+
+
+def rows_of(ref):
+    return ref[...].reshape(512, NORB)
+
+
+def early_kernel(own_ref, other_ref, rows_ref, part_ref, table_ref):
+    part_ref[...] = dot(spread(own_ref[...].astype(bf16), ((1,), (0,))), rows_of(rows_ref))
+    table_ref[...] = spread(other_ref[...].astype(bf16), ((1,), (0,)))
+
+
+def message_kernel(part_ref, table_ref, rows_ref, x_ref, out_ref):
+    green = part_ref[...] + dot(table_ref[...], rows_of(rows_ref))
+    green = green.astype(bf16).reshape(64, 8, NORB)
+    out_ref[:, 0:8, :] = green[:, :, 0:128]
+    out_ref[:, 8:16, :] = green[:, :, 128:256]
+    for i in range(64):
+        out_ref[i, 16:32, :] = x_ref[2 * ((i // 16) % 2) + (i // 4) % 2]
+
+
+def tables_kernel(table_ref, high_ref, low_ref):
+    for x, ref in zip(split(table_ref[...]), (high_ref, low_ref)):
+        ref[...] = spread(x, ((1,), (1,)))
+
+
+def back_rows(high_ref, low_ref, rows_ref):
+    rows = rows_of(rows_ref)
+    return (dot(high_ref[...], rows) + dot(low_ref[...], rows)).reshape(64, 8, NORB)
+
+
+def own_rows_kernel(high_ref, low_ref, rows_ref, out_ref):
+    own = back_rows(high_ref, low_ref, rows_ref)
+    for kk in range(2):
+        out_ref[:, kk] = own[:, 4 * kk : 4 * kk + 4].astype(bf16)
+
+
+def result_kernel(high_ref, low_ref, rows_ref, own_ref, out_ref):
+    mine = lax.axis_index("ta") % 2
+    out_ref[:, pl.ds(2 * mine, 2)] = own_ref[...]
+    other = back_rows(high_ref, low_ref, rows_ref)
+    for kk in range(2):
+        out_ref[:, 2 - 2 * mine + kk] = other[:, 4 * kk : 4 * kk + 4].astype(bf16)
 
 
 VM = pl.BlockSpec(memory_space=pltpu.VMEM)
@@ -137,9 +197,9 @@
 HALF_OUT = ((NPTS, HALF), bf16)
 
 
-def to_green(rows):
-    parts = rows.reshape(64, 2, 2, 4, 128)
-    return jnp.transpose(parts, (2, 0, 3, 1, 4)).reshape(2, NORB, NORB)
+def to_green(got):
+    rows = jnp.concatenate([got[:, 0:8], got[:, 8:16]], axis=2)
+    return rows.reshape(64, 2, 4, NORB).swapaxes(0, 1).reshape(2, NORB, NORB)
 
 
 def local(green_freq, colloc, core):
@@ -150,25 +210,27 @@
     own_w = lax.dynamic_slice_in_dim(table, c * 64, 64, 1)
     other_w = lax.dynamic_slice_in_dim(table, 64 - c * 64, 64, 1)
 
-    gf = green_freq.reshape(64, 2, 8, NORB)
-    mine = lax.dynamic_index_in_dim(gf, c, 1, keepdims=False)
-    theirs = lax.dynamic_index_in_dim(gf, 1 - c, 1, keepdims=False)
+    matrix = ((512, 512), bf16)
+    gf = green_freq.reshape(64, 2, 2, 4, NORB)
+    theirs = lax.dynamic_index_in_dim(gf, 1 - c, 1, keepdims=False).reshape(64, 8, NORB)
     arrived = lax.ppermute(theirs, "ta", CORE_SWAP)
-    part = jnp.einsum("uw,wrj->urj", own_w, mine.astype(f32), precision=lax.Precision.HIGHEST)
-    part += jnp.einsum("uw,wrj->urj", other_w, arrived.astype(f32), precision=lax.Precision.HIGHEST)
-    part = part.astype(bf16).reshape(64, 8, 2, 128).swapaxes(1, 2).reshape(64, 16, 128)
-
-    xt = jnp.swapaxes(colloc, 1, 2).reshape(2, 2, 16, 2, 128)
-    xt = lax.dynamic_index_in_dim(xt, c, 0, keepdims=False).swapaxes(1, 2).reshape(4, 16, 128)
-    xmsg = jnp.broadcast_to(xt.reshape(1, 2, 1, 2, 1, 16, 128), (2, 2, 2, 2, 4, 16, 128)).reshape(64, 16, 128)
-    got = lax.all_to_all(jnp.concatenate([part, xmsg], 1), "pa", 0, 0, tiled=True)
-    g_own = to_green(got[:, :16])
+    mine = lax.dynamic_index_in_dim(gf, c, 1, keepdims=False).reshape(64, 8, NORB)
+    part, rest = call(early_kernel, 3, (((512, NORB), f32), matrix), (), 1.0, 10)(
+        own_w, other_w, mine
+    )
+    xt = lax.dynamic_slice_in_dim(jnp.swapaxes(colloc, 1, 2), 2 * c, 2, 0)
+    xt = jnp.concatenate([xt[0:1, :, :128], xt[0:1, :, 128:], xt[1:2, :, :128], xt[1:2, :, 128:]], 0)
+    (msg,) = call(message_kernel, 4, (((64, 32, 128), bf16),), (), 0.4, 8)(part, rest, arrived, xt)
+    got = lax.all_to_all(msg, "pa", 0, 0, tiled=True)
+    g_own = to_green(got)
     xpart = got[:, 16:].reshape(NPTS, 128)
 
     g_kind = lax.ppermute(g_own, "ta", CHIP_SWAP)
     pieces = [xpart]
     for s in (1, 2, 3):
         pieces.append(lax.ppermute(xpart, ("ta", "pa"), square_pairs(s)))
+    final = own_w * jnp.where(ta < 2, 2.0, -2.0)
+    back_high, back_low = call(tables_kernel, 1, (matrix, matrix), (), 0.3, 8)(final)
     x_own = jnp.stack(pieces)
     t, own0, term0 = call(first_kernel, 3, (T_OUT, OWN_OUT, HALF_OUT), (), 1.6, 16)(x_own, g_own, g_kind)
     term0_next = lax.ppermute(term0, "ta", CORE_SWAP)
@@ -187,12 +249,11 @@
     msg = out.reshape(2, 64, 4, NORB).swapaxes(0, 1).reshape(64, 8, NORB)
     back = lax.all_to_all(msg, "pa", 0, 0, tiled=True)
     back_next = lax.ppermute(back, "ta", CORE_SWAP)
-    first = jnp.where(c == 0, back, back_next)
-    second = jnp.where(c == 0, back_next, back)
-    both = jnp.concatenate([first, second], 1)
-    final = own_w * jnp.where(ta < 2, 2.0, -2.0)
-    result = jnp.einsum("uw,urj->wrj", final, both.astype(f32), precision=lax.Precision.HIGHEST)
-    return result.astype(bf16).reshape(64, 4, 4, NORB)
+    (own_rows,) = call(own_rows_kernel, 3, (((64, 2, 4, NORB), bf16),), (), 0.3, 8)(back_high, back_low, back)
+    (result,) = call(result_kernel, 4, (((64, 4, 4, NORB), bf16),), (), 0.3, 8)(
+        back_high, back_low, back_next, own_rows
+    )
+    return result
 
 
 def solution(mesh):

time: 90.1 us -> 88 us (0.977)
  Pallas kernels: 11 us -> 14.6 us
  local copies, waits for them, and re-layouts: 4.33 us -> 1.86 us
  matrix products: 1.55 us -> 0 us
  waiting for transfers between devices: 7.78 us -> 6.39 us
  starting transfers between devices: 15.4 us -> 14.4 us
    pallas_call x0 -> x5, Pallas kernels: none -> 3.59 us  [the longest x1 1.23 us: local(): call(result_kernel, 4, (((64, 4, 4, NORB), bf16),), (), 0.3, 8)]
    reshape x6 -> x5, local copies, waits for them, and re-layouts: 3.62 us -> 0.36 us  [the longest x3 0.23 us: to_green(): return rows.reshape(64, 2, 4, NORB).swapaxes(0, 1).reshape(2, NORB, NORB)]
    dot_general x3 -> x0, matrix products: 1.55 us -> none  [the longest x1 0.7 us: local(): jnp.einsum('uw,urj->wrj', final, both.astype(f32), precision=lax.Precisio...]
    unnamed x2 -> x5, local copies, waits for them, and re-layouts: 0.01 us -> 1.23 us
    ppermute x1, waiting for transfers between devices: 1.83 us -> 0.64 us  [local(): g_kind = lax.ppermute(g_own, 'ta', CHIP_SWAP)]
    ppermute x1, waiting for transfers between devices: 1.16 us -> 0.01 us  [local(): back_next = lax.ppermute(back, 'ta', CORE_SWAP)]
    ppermute x3, waiting for transfers between devices: 3.88 us -> 4.85 us  [local(): pieces.append(lax.ppermute(xpart, ('ta', 'pa'), square_pairs(s)))]
  transfers between devices with their start and end apart: 8 -> 8, of which waited for: 7 -> 6; matrix products, arithmetic and copies ran while one was open for 2% -> 1% of each run, Pallas kernels for 4% -> 6%
where the time goes in v4:
time: 88 us; the launch traced here: 87.8 us
  blocking collectives  49.8 us (57%)
  Pallas kernels  14.6 us (17%)
  starting transfers between devices  14.4 us (16%)
  waiting for transfers between devices  6.39 us (7%)
  local copies, waits for them, and re-layouts  1.86 us (2%)
    all_to_all x1, blocking collectives, local(): got = lax.all_to_all(msg, 'pa', 0, 0, tiled=True)  31.5 us
    all_to_all x1, blocking collectives, local(): back = lax.all_to_all(msg, 'pa', 0, 0, tiled=True)  18.4 us
    pallas_call x1, Pallas kernels, local(): call(functools.partial(fourth_kernel, 512), 7, (((2, NORB, NORB), bf16),)...  5.86 us
    ppermute x3, starting transfers between devices, local(): pieces.append(lax.ppermute(xpart, ('ta', 'pa'), square_pairs(s)))  5.16 us
    ppermute x3, waiting for transfers between devices, local(): pieces.append(lax.ppermute(xpart, ('ta', 'pa'), square_pairs(s)))  4.85 us
    ppermute x1, starting transfers between devices, local(): arrived = lax.ppermute(theirs, 'ta', CORE_SWAP)  3.29 us
    ppermute x1, starting transfers between devices, local(): back_next = lax.ppermute(back, 'ta', CORE_SWAP)  2.4 us
    ppermute x1, starting transfers between devices, local(): term0_next = lax.ppermute(term0, 'ta', CORE_SWAP)  2.13 us
  transfers between devices with their start and end apart: 8, of which 6 were waited for; matrix products, arithmetic and copies ran while one was open for 1% of the time, Pallas kernels for 6%

profile of v4, /device:TPU:1, one launch (start us, length us, event | category | flops | bytes accessed | tf_op | source)
XLA Modules:
  0.0 87.8 jit_solution(1910680168567124352)
XLA Ops:
  0.0 1.2 %dynamic-slice_bitcast_fusion = (bf16[64,1,2,4,256]{4,3,2,0,1:T(4,128)(2,1)S(1)}, bf16[64,1,2,4,256]{4,3,2,0,1:T(4,128)(2,1)S(1)}) fusion(bf16[64,2,2,4,256]{4,3,2,1,0:T(4,128)(2,1)} %bitcast.28, s32[]{:T(128)S(6)} %select_n.42, s32[]{:T(128)S(6)} %select_n.41), kind=kLoop, calls=%fused_computation.4 | loop fusion | bytes 1048584
  1.3 3.3 %collective-permute-start = (bf16[64,8,256]{2,1,0:T(8,128)(2,1)S(1)}, bf16[64,8,256]{2,1,0:T(8,128)(2,1)S(1)}, u32[]{:S(2)}, u32[]{:S(2)}) collective-permute-start(bf16[64,8,256]{2,1,0:T(8,128)(2,1)S(1)} %reshape.42), channel_id=1, source_target_pairs={{0,64},{64,0},{128,192},{192,128},{1,65},{65,1},{129,193},{193,129... | collective-permute-start | bytes 786440 | tf_op jit(solution)/shard_map/ppermute | solution.py:216
  4.7 0.2 multiply_select_fusion
  4.9 0.1 broadcast_multiply_fusion
  5.0 0.8 shard_map.38
  5.9 0.3 shard_map.39
  6.2 31.5 %all_to_all.10 = bf16[64,32,128]{2,1,0:T(8,128)(2,1)S(1)} all-to-all(bf16[64,32,128]{2,1,0:T(8,128)(2,1)S(1)} %shard_map.39), channel_id=1, replica_groups=mesh['ta'=4,'pa'=64] {'pa'}, dimensions={0} | all-to-all | bytes 1048576 | tf_op jit(solution)/shard_map/all_to_all | solution.py:224
  37.7 1.2 %collective-permute-start.3 = (bf16[1024,128]{1,0:T(8,128)(2,1)S(1)}, bf16[1024,128]{1,0:T(8,128)(2,1)S(1)}, u32[]{:S(2)}, u32[]{:S(2)}) collective-permute-start(bf16[1024,128]{1,0:T(8,128)(2,1)S(1)} %bitcast.24), channel_id=1, source_target_pairs={{0,20},{1,21},{2,22},{3,23},{4,16},{5,17},{6,18},{7,19},{8,28},{9,... | collective-permute-start | bytes 786440 | tf_op jit(solution)/shard_map/ppermute | solution.py:231
  38.9 1.6 %collective-permute-start.2 = (bf16[1024,128]{1,0:T(8,128)(2,1)S(1)}, bf16[1024,128]{1,0:T(8,128)(2,1)S(1)}, u32[]{:S(2)}, u32[]{:S(2)}) collective-permute-start(bf16[1024,128]{1,0:T(8,128)(2,1)S(1)} %bitcast.25), channel_id=1, source_target_pairs={{0,16},{1,17},{2,18},{3,19},{4,20},{5,21},{6,22},{7,23},{8,24},{9,... | collective-permute-start | bytes 786440 | tf_op jit(solution)/shard_map/ppermute | solution.py:231
  40.6 2.3 %collective-permute-start.1 = (bf16[1024,128]{1,0:T(8,128)(2,1)S(1)}, bf16[1024,128]{1,0:T(8,128)(2,1)S(1)}, u32[]{:S(2)}, u32[]{:S(2)}) collective-permute-start(bf16[1024,128]{1,0:T(8,128)(2,1)S(1)} %bitcast.26), channel_id=1, source_target_pairs={{0,4},{1,5},{2,6},{3,7},{4,0},{5,1},{6,2},{7,3},{8,12},{9,13},{10,... | collective-permute-start | bytes 786440 | tf_op jit(solution)/shard_map/ppermute | solution.py:231
  43.0 0.1 copy.13
  43.1 0.1 reshape.45.g_mine
  43.2 1.1 %collective-permute-start.4 = (bf16[2,256,256]{2,1,0:T(8,128)(2,1)S(1)}, bf16[2,256,256]{2,1,0:T(8,128)(2,1)S(1)}, u32[]{:S(2)}, u32[]{:S(2)}) collective-permute-start(bf16[2,256,256]{2,1,0:T(8,128)(2,1)S(1)} %reshape.45.g_mine), channel_id=1, source_target_pairs={{0,128},{128,0},{64,192},{192,64},{1,129},{129,1},{65,193},{193,65... | collective-permute-start | bytes 786440 | tf_op jit(solution)/shard_map/ppermute | solution.py:228
  44.3 2.1 %collective-permute-done.3 = bf16[1024,128]{1,0:T(8,128)(2,1)S(1)} collective-permute-done((bf16[1024,128]{1,0:T(8,128)(2,1)S(1)}, bf16[1024,128]{1,0:T(8,128)(2,1)S(1)}, u32[]{:S(2)}, u32[]{:S(2)}) %collective-permute-start.3) | collective-permute-done | bytes 262176 | tf_op jit(solution)/shard_map/ppermute | solution.py:231
  46.4 0.9 collective-permute-done.2
  47.3 1.9 %collective-permute-done.1 = bf16[1024,128]{1,0:T(8,128)(2,1)S(1)} collective-permute-done((bf16[1024,128]{1,0:T(8,128)(2,1)S(1)}, bf16[1024,128]{1,0:T(8,128)(2,1)S(1)}, u32[]{:S(2)}, u32[]{:S(2)}) %collective-permute-start.1) | collective-permute-done | bytes 262176 | tf_op jit(solution)/shard_map/ppermute | solution.py:231
  49.1 0.1 pad_maximum_fusion.x_ref
  49.3 0.6 collective-permute-done.4.g_else
  49.9 2.0 %shard_map.40 = (bf16[4,1024,256]{2,1,0:T(8,128)(2,1)S(1)}, f32[2,1024,512]{2,1,0:T(8,128)S(1)}, bf16[1024,512]{1,0:T(8,128)(2,1)S(1)}) custom-call(bf16[4,1024,128]{2,1,0:T(8,128)(2,1)S(1)} %pad_maximum_fusion.x_ref, bf16[2,256,256]{2,1,0:T(8,128)(2,1)S(1)} %reshape.45.g_mine, bf16[2,256,256]{2,1,0:T(8,128)(2,1)S(1)} %collective-permute-done.4.g_else), custom_call_target="tpu_custom_call" | custom-call | flops 1600000000 | bytes 2097152 | tf_op jit(solution)/shard_map/pallas_call | solution.py:235
  51.9 2.1 %collective-permute-start.5 = (bf16[1024,512]{1,0:T(8,128)(2,1)S(1)}, bf16[1024,512]{1,0:T(8,128)(2,1)S(1)}, u32[]{:S(2)}, u32[]{:S(2)}) collective-permute-start(bf16[1024,512]{1,0:T(8,128)(2,1)S(1)} %get-tuple-element.18.term0), channel_id=1, source_target_pairs={{0,64},{64,0},{128,192},{192,128},{1,65},{65,1},{129,193},{193,129... | collective-permute-start | bytes 3145736 | tf_op jit(solution)/shard_map/ppermute | solution.py:236
  54.0 1.4 %shard_map.42 = (f32[2,1024,512]{2,1,0:T(8,128)S(1)}, bf16[1024,512]{1,0:T(8,128)(2,1)S(1)}) custom-call(bf16[4,1024,128]{2,1,0:T(8,128)(2,1)S(1)} %pad_maximum_fusion.x_ref, bf16[4,1024,256]{2,1,0:T(8,128)(2,1)S(1)} %get-tuple-element.19.t_ref), custom_call_target="tpu_custom_call" | custom-call | flops 1100000000 | bytes 2097152 | tf_op jit(solution)/shard_map/pallas_call | solution.py:237
  55.5 0.3 collective-permute-start.6
  55.8 0.5 collective-permute-done.5.term1
  56.3 1.7 %shard_map.41.mix0 = bf16[1024,512]{1,0:T(8,128)(2,1)S(1)} custom-call(bf16[1024,1024]{1,0:T(8,128)(2,1)S(1)} %copy-done.1, bf16[1024,512]{1,0:T(8,128)(2,1)S(1)} %get-tuple-element.18.term0, bf16[1024,512]{1,0:T(8,128)(2,1)S(1)} %collective-permute-done.5.term1), custom_call_target="tpu_custom_call" | custom-call | flops 1100000000 | bytes 2097152 | tf_op jit(solution)/shard_map/pallas_call | solution.py:239
  58.0 0.4 collective-permute-done.6.term1
  58.4 5.9 %shard_map.43 = bf16[2,256,256]{2,1,0:T(8,128)(2,1)S(1)} custom-call(bf16[1024,1024]{1,0:T(8,128)(2,1)S(1)} %copy-done.1, bf16[1024,512]{1,0:T(8,128)(2,1)S(1)} %shard_map.41.mix0, bf16[1024,512]{1,0:T(8,128)(2,1)S(1)} %get-tuple-element.20.term0, bf16[1024,512]{1,0:T(8,128)(2,1)S(1)} %collective-permute-done.6.term1, ...), custom_call_target="tpu_custom_call" | custom-call | flops 4600000000 | bytes 2097152 | tf_op jit(solution)/shard_map/pallas_call | solution.py:240
  64.3 0.1 copy.12
  64.5 18.4 %all_to_all.11.rows_ref = bf16[64,8,256]{2,1,0:T(8,128)(2,1)S(1)} all-to-all(bf16[64,8,256]{2,1,0:T(8,128)(2,1)S(1)} %reshape.47), channel_id=1, replica_groups=mesh['ta'=4,'pa'=64] {'pa'}, dimensions={0} | all-to-all | bytes 524288 | tf_op jit(solution)/shard_map/all_to_all | solution.py:250
  82.9 2.4 %collective-permute-start.7 = (bf16[64,8,256]{2,1,0:T(8,128)(2,1)S(1)}, bf16[64,8,256]{2,1,0:T(8,128)(2,1)S(1)}, u32[]{:S(2)}, u32[]{:S(2)}) collective-permute-start(bf16[64,8,256]{2,1,0:T(8,128)(2,1)S(1)} %all_to_all.11.rows_ref), channel_id=1, source_target_pairs={{0,64},{64,0},{128,192},{192,128},{1,65},{65,1},{129,193},{193,129... | collective-permute-start | bytes 786440 | tf_op jit(solution)/shard_map/ppermute | solution.py:251
  85.3 0.8 shard_map.37
  86.1 0.4 shard_map.44.own_ref
  86.6 1.2 %shard_map.45 = bf16[64,4,4,256]{3,2,1,0:T(4,128)(2,1)} custom-call(bf16[512,512]{1,0:T(8,128)(2,1)S(1)} %get-tuple-element.14.high_ref, bf16[512,512]{1,0:T(8,128)(2,1)S(1)} %get-tuple-element.15.low_ref, bf16[64,8,256]{2,1,0:T(8,128)(2,1)S(1)} %collective-permute-done.7.rows_ref, bf16[64,2,4,256]{3,2,1,0:T(4,128)(2,1)S(1)} %shard_map.44.own_ref), custom_call_target="tpu_custom_call" | custom-call | flops 300000000 | bytes 2097152 | tf_op jit(solution)/shard_map/pallas_call | solution.py:253
  (19 shorter events, 0.5 us)
Async XLA Ops:
  0.0 4.6 %copy-start = (bf16[4,256,16]{1,2,0:T(8,128)(2,1)S(1)}, bf16[4,256,16]{1,2,0:T(8,128)(2,1)}, u32[]{:S(2)}) copy-start(bf16[4,256,16]{1,2,0:T(8,128)(2,1)} %param.4) | copy-start | bytes 98308
  1.3 4.6 %collective-permute-start = (bf16[64,8,256]{2,1,0:T(8,128)(2,1)S(1)}, bf16[64,8,256]{2,1,0:T(8,128)(2,1)S(1)}, u32[]{:S(2)}, u32[]{:S(2)}) collective-permute-start(bf16[64,8,256]{2,1,0:T(8,128)(2,1)S(1)} %reshape.42), channel_id=1, source_target_pairs={{0,64},{64,0},{128,192},{192,128},{1,65},{65,1},{129,193},{193,129... | collective-permute-start | bytes 786440 | tf_op jit(solution)/shard_map/ppermute | solution.py:216
  37.7 8.7 %collective-permute-start.3 = (bf16[1024,128]{1,0:T(8,128)(2,1)S(1)}, bf16[1024,128]{1,0:T(8,128)(2,1)S(1)}, u32[]{:S(2)}, u32[]{:S(2)}) collective-permute-start(bf16[1024,128]{1,0:T(8,128)(2,1)S(1)} %bitcast.24), channel_id=1, source_target_pairs={{0,20},{1,21},{2,22},{3,23},{4,16},{5,17},{6,18},{7,19},{8,28},{9,... | collective-permute-start | bytes 786440 | tf_op jit(solution)/shard_map/ppermute | solution.py:231
  38.9 8.3 %collective-permute-start.2 = (bf16[1024,128]{1,0:T(8,128)(2,1)S(1)}, bf16[1024,128]{1,0:T(8,128)(2,1)S(1)}, u32[]{:S(2)}, u32[]{:S(2)}) collective-permute-start(bf16[1024,128]{1,0:T(8,128)(2,1)S(1)} %bitcast.25), channel_id=1, source_target_pairs={{0,16},{1,17},{2,18},{3,19},{4,20},{5,21},{6,22},{7,23},{8,24},{9,... | collective-permute-start | bytes 786440 | tf_op jit(solution)/shard_map/ppermute | solution.py:231
  40.6 8.6 %collective-permute-start.1 = (bf16[1024,128]{1,0:T(8,128)(2,1)S(1)}, bf16[1024,128]{1,0:T(8,128)(2,1)S(1)}, u32[]{:S(2)}, u32[]{:S(2)}) collective-permute-start(bf16[1024,128]{1,0:T(8,128)(2,1)S(1)} %bitcast.26), channel_id=1, source_target_pairs={{0,4},{1,5},{2,6},{3,7},{4,0},{5,1},{6,2},{7,3},{8,12},{9,13},{10,... | collective-permute-start | bytes 786440 | tf_op jit(solution)/shard_map/ppermute | solution.py:231
  43.2 6.8 %collective-permute-start.4 = (bf16[2,256,256]{2,1,0:T(8,128)(2,1)S(1)}, bf16[2,256,256]{2,1,0:T(8,128)(2,1)S(1)}, u32[]{:S(2)}, u32[]{:S(2)}) collective-permute-start(bf16[2,256,256]{2,1,0:T(8,128)(2,1)S(1)} %reshape.45.g_mine), channel_id=1, source_target_pairs={{0,128},{128,0},{64,192},{192,64},{1,129},{129,1},{65,193},{193,65... | collective-permute-start | bytes 786440 | tf_op jit(solution)/shard_map/ppermute | solution.py:228
  49.3 7.0 %copy-start.1 = (bf16[1024,1024]{1,0:T(8,128)(2,1)S(1)}, bf16[1024,1024]{1,0:T(8,128)(2,1)}, u32[]{:S(2)}) copy-start(bf16[1024,1024]{1,0:T(8,128)(2,1)} %core_ref.3) | copy-start | bytes 6291460
  51.9 4.4 %collective-permute-start.5 = (bf16[1024,512]{1,0:T(8,128)(2,1)S(1)}, bf16[1024,512]{1,0:T(8,128)(2,1)S(1)}, u32[]{:S(2)}, u32[]{:S(2)}) collective-permute-start(bf16[1024,512]{1,0:T(8,128)(2,1)S(1)} %get-tuple-element.18.term0), channel_id=1, source_target_pairs={{0,64},{64,0},{128,192},{192,128},{1,65},{65,1},{129,193},{193,129... | collective-permute-start | bytes 3145736 | tf_op jit(solution)/shard_map/ppermute | solution.py:236
  55.5 2.9 %collective-permute-start.6 = (bf16[1024,512]{1,0:T(8,128)(2,1)S(1)}, bf16[1024,512]{1,0:T(8,128)(2,1)S(1)}, u32[]{:S(2)}, u32[]{:S(2)}) collective-permute-start(bf16[1024,512]{1,0:T(8,128)(2,1)S(1)} %get-tuple-element.20.term0), channel_id=1, source_target_pairs={{0,64},{64,0},{128,192},{192,128},{1,65},{65,1},{129,193},{193,129... | collective-permute-start | bytes 3145736 | tf_op jit(solution)/shard_map/ppermute | solution.py:238
  82.9 3.7 %collective-permute-start.7 = (bf16[64,8,256]{2,1,0:T(8,128)(2,1)S(1)}, bf16[64,8,256]{2,1,0:T(8,128)(2,1)S(1)}, u32[]{:S(2)}, u32[]{:S(2)}) collective-permute-start(bf16[64,8,256]{2,1,0:T(8,128)(2,1)S(1)} %all_to_all.11.rows_ref), channel_id=1, source_target_pairs={{0,64},{64,0},{128,192},{192,128},{1,65},{65,1},{129,193},{193,129... | collective-permute-start | bytes 786440 | tf_op jit(solution)/shard_map/ppermute | solution.py:251

commit v5 on v4

--- a/solution.py
+++ b/solution.py
@@ -1,5 +1,3 @@
-import functools
-
 import jax
 import jax.numpy as jnp
 from jax import lax
@@ -47,6 +45,7 @@
 
 
 HALF = NPTS // 2
+STRIP = 512
 
 
 def square_place():
@@ -87,39 +86,28 @@
     return ((term0[...].astype(f32) + term1[...].astype(f32)) * 0.25).astype(bf16)
 
 
-def third_kernel(TW, core_ref, term0, term1, mix_ref, bub_ref):
+def mixed_columns(core_ref, term0, term1, mix_ref, bub_ref):
     bub_ref[...] = bubble_of(term0, term1)
-
-    def step(i, _):
-        rows = pl.ds(pl.multiple_of(i * TW, TW), TW)
-        mix_ref[rows, :] = dot(core_ref[rows, :], bub_ref[...]).astype(bf16)
-        return 0
-
-    lax.fori_loop(0, NPTS // TW, step, 0)
-
-
-def fourth_kernel(TW, core_ref, mix0, term0, term1, own0, own1, x_ref, out_ref, bub_ref, mix1, tmp_ref):
+    mix_ref[...] = dot(core_ref[...], bub_ref[...]).astype(bf16)
+
+
+def third_kernel(core_ref, term0, term1, mix_ref, bub_ref):
+    mixed_columns(core_ref, term0, term1, mix_ref, bub_ref)
+
+
+def fourth_kernel(core_ref, mix0, term0, term1, own0, own1, x_ref, out_ref, bub_ref, mix1, tmp_ref):
     here = square_place()
     every = pl.ds(0, NPTS)
-    third_kernel(TW, core_ref, term0, term1, mix1, bub_ref)
-
-    def step(i, _):
-        rows = pl.ds(pl.multiple_of(i * TW, TW), TW)
+    mixed_columns(core_ref, term0, term1, mix1, bub_ref)
+    for i in range(NPTS // STRIP):
+        rows = pl.ds(i * STRIP, STRIP)
         w = dot(jnp.concatenate([mix0[rows, :], mix1[rows, :]], axis=1), core_ref[...])
         for kk in range(2):
             own = jnp.concatenate([own0[kk, rows, :], own1[kk, rows, :]], axis=1)
             source = (own * w).astype(bf16)
             tmp_ref[kk, rows, :] = dot(source, points_of(x_ref, here, kk, every)).astype(bf16)
-        return 0
-
-    lax.fori_loop(0, NPTS // TW, step, 0)
     for kk in range(2):
         out_ref[kk] = dot(points_of(x_ref, here, kk, every), tmp_ref[kk], TN).astype(bf16)
-
-
-def split(x):
-    high = x.astype(bf16)
-    return high, (x - high.astype(f32)).astype(bf16)
 
 
 def one_hot(shape, which):
@@ -153,26 +141,24 @@
         out_ref[i, 16:32, :] = x_ref[2 * ((i // 16) % 2) + (i // 4) % 2]
 
 
-def tables_kernel(table_ref, high_ref, low_ref):
-    for x, ref in zip(split(table_ref[...]), (high_ref, low_ref)):
-        ref[...] = spread(x, ((1,), (1,)))
-
-
-def back_rows(high_ref, low_ref, rows_ref):
-    rows = rows_of(rows_ref)
-    return (dot(high_ref[...], rows) + dot(low_ref[...], rows)).reshape(64, 8, NORB)
-
-
-def own_rows_kernel(high_ref, low_ref, rows_ref, out_ref):
-    own = back_rows(high_ref, low_ref, rows_ref)
+def tables_kernel(table_ref, out_ref):
+    out_ref[...] = spread(table_ref[...].astype(bf16), ((1,), (1,)))
+
+
+def back_rows(table_ref, rows_ref):
+    return dot(table_ref[...], rows_of(rows_ref)).reshape(64, 8, NORB)
+
+
+def own_rows_kernel(table_ref, rows_ref, out_ref):
+    own = back_rows(table_ref, rows_ref)
     for kk in range(2):
         out_ref[:, kk] = own[:, 4 * kk : 4 * kk + 4].astype(bf16)
 
 
-def result_kernel(high_ref, low_ref, rows_ref, own_ref, out_ref):
+def result_kernel(table_ref, rows_ref, own_ref, out_ref):
     mine = lax.axis_index("ta") % 2
     out_ref[:, pl.ds(2 * mine, 2)] = own_ref[...]
-    other = back_rows(high_ref, low_ref, rows_ref)
+    other = back_rows(table_ref, rows_ref)
     for kk in range(2):
         out_ref[:, 2 - 2 * mine + kk] = other[:, 4 * kk : 4 * kk + 4].astype(bf16)
 
@@ -230,15 +216,17 @@
     for s in (1, 2, 3):
         pieces.append(lax.ppermute(xpart, ("ta", "pa"), square_pairs(s)))
     final = own_w * jnp.where(ta < 2, 2.0, -2.0)
-    back_high, back_low = call(tables_kernel, 1, (matrix, matrix), (), 0.3, 8)(final)
+    (back_table,) = call(tables_kernel, 1, (matrix,), (), 0.3, 8)(final)
     x_own = jnp.stack(pieces)
     t, own0, term0 = call(first_kernel, 3, (T_OUT, OWN_OUT, HALF_OUT), (), 1.6, 16)(x_own, g_own, g_kind)
     term0_next = lax.ppermute(term0, "ta", CORE_SWAP)
     own1, term1 = call(second_kernel, 2, (OWN_OUT, HALF_OUT), (), 1.1, 16)(x_own, t)
     term1_next = lax.ppermute(term1, "ta", CORE_SWAP)
-    (mix0,) = call(functools.partial(third_kernel, 512), 3, (HALF_OUT,), (HALF_OUT,), 1.1, 8)(core, term0, term0_next)
+    (mix0,) = call(third_kernel, 3, (HALF_OUT,), (HALF_OUT,), 1.1, 8)(
+        core, term0, term0_next
+    )
     (out,) = call(
-        functools.partial(fourth_kernel, 512),
+        fourth_kernel,
         7,
         (((2, NORB, NORB), bf16),),
         (HALF_OUT, HALF_OUT, ((2, NPTS, NORB), bf16)),
@@ -249,9 +237,9 @@
     msg = out.reshape(2, 64, 4, NORB).swapaxes(0, 1).reshape(64, 8, NORB)
     back = lax.all_to_all(msg, "pa", 0, 0, tiled=True)
     back_next = lax.ppermute(back, "ta", CORE_SWAP)
-    (own_rows,) = call(own_rows_kernel, 3, (((64, 2, 4, NORB), bf16),), (), 0.3, 8)(back_high, back_low, back)
-    (result,) = call(result_kernel, 4, (((64, 4, 4, NORB), bf16),), (), 0.3, 8)(
-        back_high, back_low, back_next, own_rows
+    (own_rows,) = call(own_rows_kernel, 2, (((64, 2, 4, NORB), bf16),), (), 0.3, 8)(back_table, back)
+    (result,) = call(result_kernel, 3, (((64, 4, 4, NORB), bf16),), (), 0.3, 8)(
+        back_table, back_next, own_rows
     )
     return result
 

time: 88 us -> 86.8 us (0.986)
  Pallas kernels: 14.6 us -> 12.6 us
    pallas_call x5, Pallas kernels: 10.1 us -> 8.09 us  [the longest x1 4.94 us: local(): call(fourth_kernel, 7, (((2, NORB, NORB), bf16),), (HALF_OUT, HALF_OUT, (...]
  transfers between devices with their start and end apart: 8 -> 8, of which waited for: 6 -> 7; matrix products, arithmetic and copies ran while one was open for 1% -> 1% of each run, Pallas kernels for 6% -> 5%
where the time goes in v5:
time: 86.8 us; the launch traced here: 86.6 us
  blocking collectives  49.9 us (57%)
  starting transfers between devices  14.4 us (17%)
  Pallas kernels  12.6 us (15%)
  waiting for transfers between devices  7.21 us (8%)
  local copies, waits for them, and re-layouts  1.86 us (2%)
    all_to_all x1, blocking collectives, local(): got = lax.all_to_all(msg, 'pa', 0, 0, tiled=True)  31.5 us
    all_to_all x1, blocking collectives, local(): back = lax.all_to_all(msg, 'pa', 0, 0, tiled=True)  18.4 us
    ppermute x3, starting transfers between devices, local(): pieces.append(lax.ppermute(xpart, ('ta', 'pa'), square_pairs(s)))  5.16 us
    pallas_call x1, Pallas kernels, local(): call(fourth_kernel, 7, (((2, NORB, NORB), bf16),), (HALF_OUT, HALF_OUT, (...  4.94 us
    ppermute x3, waiting for transfers between devices, local(): pieces.append(lax.ppermute(xpart, ('ta', 'pa'), square_pairs(s)))  4.85 us
    ppermute x1, starting transfers between devices, local(): arrived = lax.ppermute(theirs, 'ta', CORE_SWAP)  3.29 us
    ppermute x1, starting transfers between devices, local(): back_next = lax.ppermute(back, 'ta', CORE_SWAP)  2.37 us
    ppermute x1, starting transfers between devices, local(): term0_next = lax.ppermute(term0, 'ta', CORE_SWAP)  2.13 us
  transfers between devices with their start and end apart: 8, of which 7 were waited for; matrix products, arithmetic and copies ran while one was open for 1% of the time, Pallas kernels for 5%

profile of v5, /device:TPU:1, one launch (start us, length us, event | category | flops | bytes accessed | tf_op | source)
XLA Modules:
  0.0 86.6 jit_solution(17799914057655412769)
XLA Ops:
  0.0 1.2 %dynamic-slice_bitcast_fusion = (bf16[64,1,2,4,256]{4,3,2,0,1:T(4,128)(2,1)S(1)}, bf16[64,1,2,4,256]{4,3,2,0,1:T(4,128)(2,1)S(1)}) fusion(bf16[64,2,2,4,256]{4,3,2,1,0:T(4,128)(2,1)} %bitcast.28, s32[]{:T(128)S(6)} %select_n.42, s32[]{:T(128)S(6)} %select_n.41), kind=kLoop, calls=%fused_computation.4 | loop fusion | bytes 1048584
  1.3 3.3 %collective-permute-start = (bf16[64,8,256]{2,1,0:T(8,128)(2,1)S(1)}, bf16[64,8,256]{2,1,0:T(8,128)(2,1)S(1)}, u32[]{:S(2)}, u32[]{:S(2)}) collective-permute-start(bf16[64,8,256]{2,1,0:T(8,128)(2,1)S(1)} %reshape.42), channel_id=1, source_target_pairs={{0,64},{64,0},{128,192},{192,128},{1,65},{65,1},{129,193},{193,129... | collective-permute-start | bytes 786440 | tf_op jit(solution)/shard_map/ppermute | solution.py:202
  4.7 0.2 multiply_select_fusion
  4.9 0.1 broadcast_multiply_fusion
  5.0 0.8 shard_map.38
  5.9 0.3 shard_map.39
  6.2 31.5 %all_to_all.10 = bf16[64,32,128]{2,1,0:T(8,128)(2,1)S(1)} all-to-all(bf16[64,32,128]{2,1,0:T(8,128)(2,1)S(1)} %shard_map.39), channel_id=1, replica_groups=mesh['ta'=4,'pa'=64] {'pa'}, dimensions={0} | all-to-all | bytes 1048576 | tf_op jit(solution)/shard_map/all_to_all | solution.py:210
  37.7 1.2 %collective-permute-start.3 = (bf16[1024,128]{1,0:T(8,128)(2,1)S(1)}, bf16[1024,128]{1,0:T(8,128)(2,1)S(1)}, u32[]{:S(2)}, u32[]{:S(2)}) collective-permute-start(bf16[1024,128]{1,0:T(8,128)(2,1)S(1)} %bitcast.24), channel_id=1, source_target_pairs={{0,20},{1,21},{2,22},{3,23},{4,16},{5,17},{6,18},{7,19},{8,28},{9,... | collective-permute-start | bytes 786440 | tf_op jit(solution)/shard_map/ppermute | solution.py:217
  38.9 1.6 %collective-permute-start.2 = (bf16[1024,128]{1,0:T(8,128)(2,1)S(1)}, bf16[1024,128]{1,0:T(8,128)(2,1)S(1)}, u32[]{:S(2)}, u32[]{:S(2)}) collective-permute-start(bf16[1024,128]{1,0:T(8,128)(2,1)S(1)} %bitcast.25), channel_id=1, source_target_pairs={{0,16},{1,17},{2,18},{3,19},{4,20},{5,21},{6,22},{7,23},{8,24},{9,... | collective-permute-start | bytes 786440 | tf_op jit(solution)/shard_map/ppermute | solution.py:217
  40.6 2.3 %collective-permute-start.1 = (bf16[1024,128]{1,0:T(8,128)(2,1)S(1)}, bf16[1024,128]{1,0:T(8,128)(2,1)S(1)}, u32[]{:S(2)}, u32[]{:S(2)}) collective-permute-start(bf16[1024,128]{1,0:T(8,128)(2,1)S(1)} %bitcast.26), channel_id=1, source_target_pairs={{0,4},{1,5},{2,6},{3,7},{4,0},{5,1},{6,2},{7,3},{8,12},{9,13},{10,... | collective-permute-start | bytes 786440 | tf_op jit(solution)/shard_map/ppermute | solution.py:217
  43.0 0.1 copy.13
  43.2 1.1 %collective-permute-start.4 = (bf16[2,256,256]{2,1,0:T(8,128)(2,1)S(1)}, bf16[2,256,256]{2,1,0:T(8,128)(2,1)S(1)}, u32[]{:S(2)}, u32[]{:S(2)}) collective-permute-start(bf16[2,256,256]{2,1,0:T(8,128)(2,1)S(1)} %reshape.45.g_mine), channel_id=1, source_target_pairs={{0,128},{128,0},{64,192},{192,64},{1,129},{129,1},{65,193},{193,65... | collective-permute-start | bytes 786440 | tf_op jit(solution)/shard_map/ppermute | solution.py:214
  44.3 2.1 %collective-permute-done.3 = bf16[1024,128]{1,0:T(8,128)(2,1)S(1)} collective-permute-done((bf16[1024,128]{1,0:T(8,128)(2,1)S(1)}, bf16[1024,128]{1,0:T(8,128)(2,1)S(1)}, u32[]{:S(2)}, u32[]{:S(2)}) %collective-permute-start.3) | collective-permute-done | bytes 262176 | tf_op jit(solution)/shard_map/ppermute | solution.py:217
  46.4 0.9 collective-permute-done.2
  47.3 1.9 %collective-permute-done.1 = bf16[1024,128]{1,0:T(8,128)(2,1)S(1)} collective-permute-done((bf16[1024,128]{1,0:T(8,128)(2,1)S(1)}, bf16[1024,128]{1,0:T(8,128)(2,1)S(1)}, u32[]{:S(2)}, u32[]{:S(2)}) %collective-permute-start.1) | collective-permute-done | bytes 262176 | tf_op jit(solution)/shard_map/ppermute | solution.py:217
  49.1 0.1 pad_maximum_fusion.x_ref
  49.3 0.6 collective-permute-done.4.g_else
  49.9 2.0 %shard_map.40 = (bf16[4,1024,256]{2,1,0:T(8,128)(2,1)S(1)}, f32[2,1024,512]{2,1,0:T(8,128)S(1)}, bf16[1024,512]{1,0:T(8,128)(2,1)S(1)}) custom-call(bf16[4,1024,128]{2,1,0:T(8,128)(2,1)S(1)} %pad_maximum_fusion.x_ref, bf16[2,256,256]{2,1,0:T(8,128)(2,1)S(1)} %reshape.45.g_mine, bf16[2,256,256]{2,1,0:T(8,128)(2,1)S(1)} %collective-permute-done.4.g_else), custom_call_target="tpu_custom_call" | custom-call | flops 1600000000 | bytes 2097152 | tf_op jit(solution)/shard_map/pallas_call | solution.py:221
  51.9 2.1 %collective-permute-start.5 = (bf16[1024,512]{1,0:T(8,128)(2,1)S(1)}, bf16[1024,512]{1,0:T(8,128)(2,1)S(1)}, u32[]{:S(2)}, u32[]{:S(2)}) collective-permute-start(bf16[1024,512]{1,0:T(8,128)(2,1)S(1)} %get-tuple-element.14.term0), channel_id=1, source_target_pairs={{0,64},{64,0},{128,192},{192,128},{1,65},{65,1},{129,193},{193,129... | collective-permute-start | bytes 3145736 | tf_op jit(solution)/shard_map/ppermute | solution.py:222
  54.0 1.4 %shard_map.42 = (f32[2,1024,512]{2,1,0:T(8,128)S(1)}, bf16[1024,512]{1,0:T(8,128)(2,1)S(1)}) custom-call(bf16[4,1024,128]{2,1,0:T(8,128)(2,1)S(1)} %pad_maximum_fusion.x_ref, bf16[4,1024,256]{2,1,0:T(8,128)(2,1)S(1)} %get-tuple-element.15.t_ref), custom_call_target="tpu_custom_call" | custom-call | flops 1100000000 | bytes 2097152 | tf_op jit(solution)/shard_map/pallas_call | solution.py:223
  55.5 0.3 collective-permute-start.6
  55.8 0.5 collective-permute-done.5.term1
  56.3 1.3 %shard_map.41.mix0 = bf16[1024,512]{1,0:T(8,128)(2,1)S(1)} custom-call(bf16[1024,1024]{1,0:T(8,128)(2,1)S(1)} %copy-done.1, bf16[1024,512]{1,0:T(8,128)(2,1)S(1)} %get-tuple-element.14.term0, bf16[1024,512]{1,0:T(8,128)(2,1)S(1)} %collective-permute-done.5.term1), custom_call_target="tpu_custom_call" | custom-call | flops 1100000000 | bytes 2097152 | tf_op jit(solution)/shard_map/pallas_call | solution.py:225
  57.6 0.8 collective-permute-done.6.term1
  58.4 4.9 %shard_map.43 = bf16[2,256,256]{2,1,0:T(8,128)(2,1)S(1)} custom-call(bf16[1024,1024]{1,0:T(8,128)(2,1)S(1)} %copy-done.1, bf16[1024,512]{1,0:T(8,128)(2,1)S(1)} %shard_map.41.mix0, bf16[1024,512]{1,0:T(8,128)(2,1)S(1)} %get-tuple-element.16.term0, bf16[1024,512]{1,0:T(8,128)(2,1)S(1)} %collective-permute-done.6.term1, ...), custom_call_target="tpu_custom_call" | custom-call | flops 4600000000 | bytes 2097152 | tf_op jit(solution)/shard_map/pallas_call | solution.py:228
  63.4 0.1 copy.12
  63.6 18.4 %all_to_all.11.rows_ref = bf16[64,8,256]{2,1,0:T(8,128)(2,1)S(1)} all-to-all(bf16[64,8,256]{2,1,0:T(8,128)(2,1)S(1)} %reshape.47), channel_id=1, replica_groups=mesh['ta'=4,'pa'=64] {'pa'}, dimensions={0} | all-to-all | bytes 524288 | tf_op jit(solution)/shard_map/all_to_all | solution.py:238
  82.0 2.4 %collective-permute-start.7 = (bf16[64,8,256]{2,1,0:T(8,128)(2,1)S(1)}, bf16[64,8,256]{2,1,0:T(8,128)(2,1)S(1)}, u32[]{:S(2)}, u32[]{:S(2)}) collective-permute-start(bf16[64,8,256]{2,1,0:T(8,128)(2,1)S(1)} %all_to_all.11.rows_ref), channel_id=1, source_target_pairs={{0,64},{64,0},{128,192},{192,128},{1,65},{65,1},{129,193},{193,129... | collective-permute-start | bytes 786440 | tf_op jit(solution)/shard_map/ppermute | solution.py:239
  84.3 0.5 shard_map.37.table_ref
  84.8 0.3 shard_map.44.own_ref
  85.1 0.4 collective-permute-done.7.rows_ref
  85.5 1.1 %shard_map.45 = bf16[64,4,4,256]{3,2,1,0:T(4,128)(2,1)} custom-call(bf16[512,512]{1,0:T(8,128)(2,1)S(1)} %shard_map.37.table_ref, bf16[64,8,256]{2,1,0:T(8,128)(2,1)S(1)} %collective-permute-done.7.rows_ref, bf16[64,2,4,256]{3,2,1,0:T(4,128)(2,1)S(1)} %shard_map.44.own_ref), custom_call_target="tpu_custom_call" | custom-call | flops 300000000 | bytes 2097152 | tf_op jit(solution)/shard_map/pallas_call | solution.py:241
  (19 shorter events, 0.5 us)
Async XLA Ops:
  0.0 4.6 %copy-start = (bf16[4,256,16]{1,2,0:T(8,128)(2,1)S(1)}, bf16[4,256,16]{1,2,0:T(8,128)(2,1)}, u32[]{:S(2)}) copy-start(bf16[4,256,16]{1,2,0:T(8,128)(2,1)} %param.4) | copy-start | bytes 98308
  1.3 4.6 %collective-permute-start = (bf16[64,8,256]{2,1,0:T(8,128)(2,1)S(1)}, bf16[64,8,256]{2,1,0:T(8,128)(2,1)S(1)}, u32[]{:S(2)}, u32[]{:S(2)}) collective-permute-start(bf16[64,8,256]{2,1,0:T(8,128)(2,1)S(1)} %reshape.42), channel_id=1, source_target_pairs={{0,64},{64,0},{128,192},{192,128},{1,65},{65,1},{129,193},{193,129... | collective-permute-start | bytes 786440 | tf_op jit(solution)/shard_map/ppermute | solution.py:202
  37.7 8.7 %collective-permute-start.3 = (bf16[1024,128]{1,0:T(8,128)(2,1)S(1)}, bf16[1024,128]{1,0:T(8,128)(2,1)S(1)}, u32[]{:S(2)}, u32[]{:S(2)}) collective-permute-start(bf16[1024,128]{1,0:T(8,128)(2,1)S(1)} %bitcast.24), channel_id=1, source_target_pairs={{0,20},{1,21},{2,22},{3,23},{4,16},{5,17},{6,18},{7,19},{8,28},{9,... | collective-permute-start | bytes 786440 | tf_op jit(solution)/shard_map/ppermute | solution.py:217
  38.9 8.3 %collective-permute-start.2 = (bf16[1024,128]{1,0:T(8,128)(2,1)S(1)}, bf16[1024,128]{1,0:T(8,128)(2,1)S(1)}, u32[]{:S(2)}, u32[]{:S(2)}) collective-permute-start(bf16[1024,128]{1,0:T(8,128)(2,1)S(1)} %bitcast.25), channel_id=1, source_target_pairs={{0,16},{1,17},{2,18},{3,19},{4,20},{5,21},{6,22},{7,23},{8,24},{9,... | collective-permute-start | bytes 786440 | tf_op jit(solution)/shard_map/ppermute | solution.py:217
  40.6 8.6 %collective-permute-start.1 = (bf16[1024,128]{1,0:T(8,128)(2,1)S(1)}, bf16[1024,128]{1,0:T(8,128)(2,1)S(1)}, u32[]{:S(2)}, u32[]{:S(2)}) collective-permute-start(bf16[1024,128]{1,0:T(8,128)(2,1)S(1)} %bitcast.26), channel_id=1, source_target_pairs={{0,4},{1,5},{2,6},{3,7},{4,0},{5,1},{6,2},{7,3},{8,12},{9,13},{10,... | collective-permute-start | bytes 786440 | tf_op jit(solution)/shard_map/ppermute | solution.py:217
  43.2 6.8 %collective-permute-start.4 = (bf16[2,256,256]{2,1,0:T(8,128)(2,1)S(1)}, bf16[2,256,256]{2,1,0:T(8,128)(2,1)S(1)}, u32[]{:S(2)}, u32[]{:S(2)}) collective-permute-start(bf16[2,256,256]{2,1,0:T(8,128)(2,1)S(1)} %reshape.45.g_mine), channel_id=1, source_target_pairs={{0,128},{128,0},{64,192},{192,64},{1,129},{129,1},{65,193},{193,65... | collective-permute-start | bytes 786440 | tf_op jit(solution)/shard_map/ppermute | solution.py:214
  49.3 7.0 %copy-start.1 = (bf16[1024,1024]{1,0:T(8,128)(2,1)S(1)}, bf16[1024,1024]{1,0:T(8,128)(2,1)}, u32[]{:S(2)}) copy-start(bf16[1024,1024]{1,0:T(8,128)(2,1)} %core_ref.3) | copy-start | bytes 6291460
  51.9 4.4 %collective-permute-start.5 = (bf16[1024,512]{1,0:T(8,128)(2,1)S(1)}, bf16[1024,512]{1,0:T(8,128)(2,1)S(1)}, u32[]{:S(2)}, u32[]{:S(2)}) collective-permute-start(bf16[1024,512]{1,0:T(8,128)(2,1)S(1)} %get-tuple-element.14.term0), channel_id=1, source_target_pairs={{0,64},{64,0},{128,192},{192,128},{1,65},{65,1},{129,193},{193,129... | collective-permute-start | bytes 3145736 | tf_op jit(solution)/shard_map/ppermute | solution.py:222
  55.5 2.9 %collective-permute-start.6 = (bf16[1024,512]{1,0:T(8,128)(2,1)S(1)}, bf16[1024,512]{1,0:T(8,128)(2,1)S(1)}, u32[]{:S(2)}, u32[]{:S(2)}) collective-permute-start(bf16[1024,512]{1,0:T(8,128)(2,1)S(1)} %get-tuple-element.16.term0), channel_id=1, source_target_pairs={{0,64},{64,0},{128,192},{192,128},{1,65},{65,1},{129,193},{193,129... | collective-permute-start | bytes 3145736 | tf_op jit(solution)/shard_map/ppermute | solution.py:224
  82.0 3.5 %collective-permute-start.7 = (bf16[64,8,256]{2,1,0:T(8,128)(2,1)S(1)}, bf16[64,8,256]{2,1,0:T(8,128)(2,1)S(1)}, u32[]{:S(2)}, u32[]{:S(2)}) collective-permute-start(bf16[64,8,256]{2,1,0:T(8,128)(2,1)S(1)} %all_to_all.11.rows_ref), channel_id=1, source_target_pairs={{0,64},{64,0},{128,192},{192,128},{1,65},{65,1},{129,193},{193,129... | collective-permute-start | bytes 786440 | tf_op jit(solution)/shard_map/ppermute | solution.py:239

commit v6 on v5

--- a/solution.py
+++ b/solution.py
@@ -106,8 +106,8 @@
             own = jnp.concatenate([own0[kk, rows, :], own1[kk, rows, :]], axis=1)
             source = (own * w).astype(bf16)
             tmp_ref[kk, rows, :] = dot(source, points_of(x_ref, here, kk, every)).astype(bf16)
-    for kk in range(2):
-        out_ref[kk] = dot(points_of(x_ref, here, kk, every), tmp_ref[kk], TN).astype(bf16)
+    rows = [dot(points_of(x_ref, here, kk, every), tmp_ref[kk], TN).reshape(64, 4, NORB) for kk in range(2)]
+    out_ref[...] = jnp.concatenate(rows, axis=1).astype(bf16)
 
 
 def one_hot(shape, which):
@@ -211,7 +211,7 @@
     g_own = to_green(got)
     xpart = got[:, 16:].reshape(NPTS, 128)
 
-    g_kind = lax.ppermute(g_own, "ta", CHIP_SWAP)
+    g_kind = to_green(lax.ppermute(got[:, :16], "ta", CHIP_SWAP))
     pieces = [xpart]
     for s in (1, 2, 3):
         pieces.append(lax.ppermute(xpart, ("ta", "pa"), square_pairs(s)))
@@ -228,14 +228,13 @@
     (out,) = call(
         fourth_kernel,
         7,
-        (((2, NORB, NORB), bf16),),
+        (((64, 8, NORB), bf16),),
         (HALF_OUT, HALF_OUT, ((2, NPTS, NORB), bf16)),
         4.6,
         20,
     )(core, mix0, term1, term1_next, own0, own1, x_own)
 
-    msg = out.reshape(2, 64, 4, NORB).swapaxes(0, 1).reshape(64, 8, NORB)
-    back = lax.all_to_all(msg, "pa", 0, 0, tiled=True)
+    back = lax.all_to_all(out, "pa", 0, 0, tiled=True)
     back_next = lax.ppermute(back, "ta", CORE_SWAP)
     (own_rows,) = call(own_rows_kernel, 2, (((64, 2, 4, NORB), bf16),), (), 0.3, 8)(back_table, back)
     (result,) = call(result_kernel, 3, (((64, 4, 4, NORB), bf16),), (), 0.3, 8)(

time: 86.8 us -> 86.6 us (level)
    ppermute x3, waiting for transfers between devices: 4.85 us -> 0.01 us  [local(): pieces.append(lax.ppermute(xpart, ('ta', 'pa'), square_pairs(s)))]
    ppermute x1, waiting for transfers between devices: 0.64 us -> 5.33 us  [local(): g_kind = to_green(lax.ppermute(got[:, :16], 'ta', CHIP_SWAP))]
  transfers between devices with their start and end apart: 8 -> 8, of which waited for: 7 -> 4; matrix products, arithmetic and copies ran while one was open for 1% -> 1% of each run, Pallas kernels for 5% -> 5%
where the time goes in v6:
time: 86.6 us; the launch traced here: 86.5 us
  blocking collectives  49.9 us (58%)
  starting transfers between devices  14.3 us (17%)
  Pallas kernels  12.6 us (15%)
  waiting for transfers between devices  7.06 us (8%)
  local copies, waits for them, and re-layouts  1.9 us (2%)
    all_to_all x1, blocking collectives, local(): got = lax.all_to_all(msg, 'pa', 0, 0, tiled=True)  31.5 us
    all_to_all x1, blocking collectives, local(): back = lax.all_to_all(out, 'pa', 0, 0, tiled=True)  18.4 us
    ppermute x1, waiting for transfers between devices, local(): g_kind = to_green(lax.ppermute(got[:, :16], 'ta', CHIP_SWAP))  5.33 us
    ppermute x3, starting transfers between devices, local(): pieces.append(lax.ppermute(xpart, ('ta', 'pa'), square_pairs(s)))  5.16 us
    pallas_call x1, Pallas kernels, local(): call(fourth_kernel, 7, (((64, 8, NORB), bf16),), (HALF_OUT, HALF_OUT, ((2...  4.95 us
    ppermute x1, starting transfers between devices, local(): arrived = lax.ppermute(theirs, 'ta', CORE_SWAP)  3.29 us
    ppermute x1, starting transfers between devices, local(): back_next = lax.ppermute(back, 'ta', CORE_SWAP)  2.37 us
    ppermute x1, starting transfers between devices, local(): term0_next = lax.ppermute(term0, 'ta', CORE_SWAP)  2.13 us
  transfers between devices with their start and end apart: 8, of which 4 were waited for; matrix products, arithmetic and copies ran while one was open for 1% of the time, Pallas kernels for 5%

profile of v6, /device:TPU:1, one launch (start us, length us, event | category | flops | bytes accessed | tf_op | source)
XLA Modules:
  0.0 86.5 jit_solution(11001616772690328406)
XLA Ops:
  0.0 1.2 %dynamic-slice_bitcast_fusion = (bf16[64,1,2,4,256]{4,3,2,0,1:T(4,128)(2,1)S(1)}, bf16[64,1,2,4,256]{4,3,2,0,1:T(4,128)(2,1)S(1)}) fusion(bf16[64,2,2,4,256]{4,3,2,1,0:T(4,128)(2,1)} %bitcast.28, s32[]{:T(128)S(6)} %select_n.42, s32[]{:T(128)S(6)} %select_n.41), kind=kLoop, calls=%fused_computation.5 | loop fusion | bytes 1048584
  1.2 0.1 reshape.42
  1.3 3.3 %collective-permute-start = (bf16[64,8,256]{2,1,0:T(8,128)(2,1)S(1)}, bf16[64,8,256]{2,1,0:T(8,128)(2,1)S(1)}, u32[]{:S(2)}, u32[]{:S(2)}) collective-permute-start(bf16[64,8,256]{2,1,0:T(8,128)(2,1)S(1)} %reshape.42), channel_id=1, source_target_pairs={{0,64},{64,0},{128,192},{192,128},{1,65},{65,1},{129,193},{193,129... | collective-permute-start | bytes 786440 | tf_op jit(solution)/shard_map/ppermute | solution.py:202
  4.7 0.2 multiply_select_fusion
  4.9 0.1 broadcast_multiply_fusion
  5.0 0.1 reshape.41.rows_ref
  5.0 0.8 shard_map.38
  5.9 0.3 shard_map.39
  6.2 31.5 %all_to_all.10 = bf16[64,32,128]{2,1,0:T(8,128)(2,1)S(1)} all-to-all(bf16[64,32,128]{2,1,0:T(8,128)(2,1)S(1)} %shard_map.39), channel_id=1, replica_groups=mesh['ta'=4,'pa'=64] {'pa'}, dimensions={0} | all-to-all | bytes 1048576 | tf_op jit(solution)/shard_map/all_to_all | solution.py:210
  37.7 1.2 %collective-permute-start.3 = (bf16[1024,128]{1,0:T(8,128)(2,1)S(1)}, bf16[1024,128]{1,0:T(8,128)(2,1)S(1)}, u32[]{:S(2)}, u32[]{:S(2)}) collective-permute-start(bf16[1024,128]{1,0:T(8,128)(2,1)S(1)} %bitcast.24), channel_id=1, source_target_pairs={{0,20},{1,21},{2,22},{3,23},{4,16},{5,17},{6,18},{7,19},{8,28},{9,... | collective-permute-start | bytes 786440 | tf_op jit(solution)/shard_map/ppermute | solution.py:217
  39.0 1.6 %collective-permute-start.2 = (bf16[1024,128]{1,0:T(8,128)(2,1)S(1)}, bf16[1024,128]{1,0:T(8,128)(2,1)S(1)}, u32[]{:S(2)}, u32[]{:S(2)}) collective-permute-start(bf16[1024,128]{1,0:T(8,128)(2,1)S(1)} %bitcast.25), channel_id=1, source_target_pairs={{0,16},{1,17},{2,18},{3,19},{4,20},{5,21},{6,22},{7,23},{8,24},{9,... | collective-permute-start | bytes 786440 | tf_op jit(solution)/shard_map/ppermute | solution.py:217
  40.6 2.3 %collective-permute-start.1 = (bf16[1024,128]{1,0:T(8,128)(2,1)S(1)}, bf16[1024,128]{1,0:T(8,128)(2,1)S(1)}, u32[]{:S(2)}, u32[]{:S(2)}) collective-permute-start(bf16[1024,128]{1,0:T(8,128)(2,1)S(1)} %bitcast.26), channel_id=1, source_target_pairs={{0,4},{1,5},{2,6},{3,7},{4,0},{5,1},{6,2},{7,3},{8,12},{9,13},{10,... | collective-permute-start | bytes 786440 | tf_op jit(solution)/shard_map/ppermute | solution.py:217
  42.9 1.0 %collective-permute-start.4 = (bf16[64,16,128]{2,1,0:T(8,128)(2,1)S(1)}, bf16[64,16,128]{2,1,0:T(8,128)(2,1)S(1)}, u32[]{:S(2)}, u32[]{:S(2)}) collective-permute-start(bf16[64,16,128]{2,1,0:T(8,128)(2,1)S(1)} %get-tuple-element.21), channel_id=1, source_target_pairs={{0,128},{128,0},{64,192},{192,64},{1,129},{129,1},{65,193},{193,65... | collective-permute-start | bytes 786440 | tf_op jit(solution)/shard_map/ppermute | solution.py:214
  44.0 0.1 reshape.44
  44.0 0.1 copy.13
  44.2 5.3 %collective-permute-done.4 = bf16[64,16,128]{2,1,0:T(8,128)(2,1)S(1)} collective-permute-done((bf16[64,16,128]{2,1,0:T(8,128)(2,1)S(1)}, bf16[64,16,128]{2,1,0:T(8,128)(2,1)S(1)}, u32[]{:S(2)}, u32[]{:S(2)}) %collective-permute-start.4) | collective-permute-done | bytes 262176 | tf_op jit(solution)/shard_map/ppermute | solution.py:214
  49.7 0.1 copy.12
  49.9 0.1 pad_maximum_fusion.x_ref
  50.0 2.0 %shard_map.40 = (bf16[4,1024,256]{2,1,0:T(8,128)(2,1)S(1)}, f32[2,1024,512]{2,1,0:T(8,128)S(1)}, bf16[1024,512]{1,0:T(8,128)(2,1)S(1)}) custom-call(bf16[4,1024,128]{2,1,0:T(8,128)(2,1)S(1)} %pad_maximum_fusion.x_ref, bf16[2,256,256]{2,1,0:T(8,128)(2,1)S(1)} %reshape.45.g_mine, bf16[2,256,256]{2,1,0:T(8,128)(2,1)S(1)} %reshape.47.g_else), custom_call_target="tpu_custom_call" | custom-call | flops 1600000000 | bytes 2097152 | tf_op jit(solution)/shard_map/pallas_call | solution.py:221
  52.0 2.1 %collective-permute-start.5 = (bf16[1024,512]{1,0:T(8,128)(2,1)S(1)}, bf16[1024,512]{1,0:T(8,128)(2,1)S(1)}, u32[]{:S(2)}, u32[]{:S(2)}) collective-permute-start(bf16[1024,512]{1,0:T(8,128)(2,1)S(1)} %get-tuple-element.14.term0), channel_id=1, source_target_pairs={{0,64},{64,0},{128,192},{192,128},{1,65},{65,1},{129,193},{193,129... | collective-permute-start | bytes 3145736 | tf_op jit(solution)/shard_map/ppermute | solution.py:222
  54.1 1.4 %shard_map.42 = (f32[2,1024,512]{2,1,0:T(8,128)S(1)}, bf16[1024,512]{1,0:T(8,128)(2,1)S(1)}) custom-call(bf16[4,1024,128]{2,1,0:T(8,128)(2,1)S(1)} %pad_maximum_fusion.x_ref, bf16[4,1024,256]{2,1,0:T(8,128)(2,1)S(1)} %get-tuple-element.15.t_ref), custom_call_target="tpu_custom_call" | custom-call | flops 1100000000 | bytes 2097152 | tf_op jit(solution)/shard_map/pallas_call | solution.py:223
  55.6 0.3 collective-permute-start.6
  55.9 0.5 collective-permute-done.5.term1
  56.4 1.3 %shard_map.41.mix0 = bf16[1024,512]{1,0:T(8,128)(2,1)S(1)} custom-call(bf16[1024,1024]{1,0:T(8,128)(2,1)S(1)} %copy-done.1, bf16[1024,512]{1,0:T(8,128)(2,1)S(1)} %get-tuple-element.14.term0, bf16[1024,512]{1,0:T(8,128)(2,1)S(1)} %collective-permute-done.5.term1), custom_call_target="tpu_custom_call" | custom-call | flops 1100000000 | bytes 2097152 | tf_op jit(solution)/shard_map/pallas_call | solution.py:225
  57.7 0.8 collective-permute-done.6.term1
  58.5 4.9 %shard_map.43 = bf16[64,8,256]{2,1,0:T(8,128)(2,1)S(1)} custom-call(bf16[1024,1024]{1,0:T(8,128)(2,1)S(1)} %copy-done.1, bf16[1024,512]{1,0:T(8,128)(2,1)S(1)} %shard_map.41.mix0, bf16[1024,512]{1,0:T(8,128)(2,1)S(1)} %get-tuple-element.16.term0, bf16[1024,512]{1,0:T(8,128)(2,1)S(1)} %collective-permute-done.6.term1, ...), custom_call_target="tpu_custom_call" | custom-call | flops 4600000000 | bytes 2097152 | tf_op jit(solution)/shard_map/pallas_call | solution.py:228
  63.5 18.4 %all_to_all.11.rows_ref = bf16[64,8,256]{2,1,0:T(8,128)(2,1)S(1)} all-to-all(bf16[64,8,256]{2,1,0:T(8,128)(2,1)S(1)} %shard_map.43), channel_id=1, replica_groups=mesh['ta'=4,'pa'=64] {'pa'}, dimensions={0} | all-to-all | bytes 524288 | tf_op jit(solution)/shard_map/all_to_all | solution.py:237
  81.9 2.4 %collective-permute-start.7 = (bf16[64,8,256]{2,1,0:T(8,128)(2,1)S(1)}, bf16[64,8,256]{2,1,0:T(8,128)(2,1)S(1)}, u32[]{:S(2)}, u32[]{:S(2)}) collective-permute-start(bf16[64,8,256]{2,1,0:T(8,128)(2,1)S(1)} %all_to_all.11.rows_ref), channel_id=1, source_target_pairs={{0,64},{64,0},{128,192},{192,128},{1,65},{65,1},{129,193},{193,129... | collective-permute-start | bytes 786440 | tf_op jit(solution)/shard_map/ppermute | solution.py:238
  84.2 0.5 shard_map.37.table_ref
  84.7 0.3 shard_map.44.own_ref
  85.0 0.4 collective-permute-done.7.rows_ref
  85.4 1.1 %shard_map.45 = bf16[64,4,4,256]{3,2,1,0:T(4,128)(2,1)} custom-call(bf16[512,512]{1,0:T(8,128)(2,1)S(1)} %shard_map.37.table_ref, bf16[64,8,256]{2,1,0:T(8,128)(2,1)S(1)} %collective-permute-done.7.rows_ref, bf16[64,2,4,256]{3,2,1,0:T(4,128)(2,1)S(1)} %shard_map.44.own_ref), custom_call_target="tpu_custom_call" | custom-call | flops 300000000 | bytes 2097152 | tf_op jit(solution)/shard_map/pallas_call | solution.py:240
  (21 shorter events, 0.4 us)
Async XLA Ops:
  0.0 4.6 %copy-start = (bf16[4,256,16]{1,2,0:T(8,128)(2,1)S(1)}, bf16[4,256,16]{1,2,0:T(8,128)(2,1)}, u32[]{:S(2)}) copy-start(bf16[4,256,16]{1,2,0:T(8,128)(2,1)} %param.4) | copy-start | bytes 98308
  1.3 4.6 %collective-permute-start = (bf16[64,8,256]{2,1,0:T(8,128)(2,1)S(1)}, bf16[64,8,256]{2,1,0:T(8,128)(2,1)S(1)}, u32[]{:S(2)}, u32[]{:S(2)}) collective-permute-start(bf16[64,8,256]{2,1,0:T(8,128)(2,1)S(1)} %reshape.42), channel_id=1, source_target_pairs={{0,64},{64,0},{128,192},{192,128},{1,65},{65,1},{129,193},{193,129... | collective-permute-start | bytes 786440 | tf_op jit(solution)/shard_map/ppermute | solution.py:202
  37.7 12.1 %collective-permute-start.3 = (bf16[1024,128]{1,0:T(8,128)(2,1)S(1)}, bf16[1024,128]{1,0:T(8,128)(2,1)S(1)}, u32[]{:S(2)}, u32[]{:S(2)}) collective-permute-start(bf16[1024,128]{1,0:T(8,128)(2,1)S(1)} %bitcast.24), channel_id=1, source_target_pairs={{0,20},{1,21},{2,22},{3,23},{4,16},{5,17},{6,18},{7,19},{8,28},{9,... | collective-permute-start | bytes 786440 | tf_op jit(solution)/shard_map/ppermute | solution.py:217
  39.0 10.9 %collective-permute-start.2 = (bf16[1024,128]{1,0:T(8,128)(2,1)S(1)}, bf16[1024,128]{1,0:T(8,128)(2,1)S(1)}, u32[]{:S(2)}, u32[]{:S(2)}) collective-permute-start(bf16[1024,128]{1,0:T(8,128)(2,1)S(1)} %bitcast.25), channel_id=1, source_target_pairs={{0,16},{1,17},{2,18},{3,19},{4,20},{5,21},{6,22},{7,23},{8,24},{9,... | collective-permute-start | bytes 786440 | tf_op jit(solution)/shard_map/ppermute | solution.py:217
  40.6 9.3 %collective-permute-start.1 = (bf16[1024,128]{1,0:T(8,128)(2,1)S(1)}, bf16[1024,128]{1,0:T(8,128)(2,1)S(1)}, u32[]{:S(2)}, u32[]{:S(2)}) collective-permute-start(bf16[1024,128]{1,0:T(8,128)(2,1)S(1)} %bitcast.26), channel_id=1, source_target_pairs={{0,4},{1,5},{2,6},{3,7},{4,0},{5,1},{6,2},{7,3},{8,12},{9,13},{10,... | collective-permute-start | bytes 786440 | tf_op jit(solution)/shard_map/ppermute | solution.py:217
  42.9 6.7 %collective-permute-start.4 = (bf16[64,16,128]{2,1,0:T(8,128)(2,1)S(1)}, bf16[64,16,128]{2,1,0:T(8,128)(2,1)S(1)}, u32[]{:S(2)}, u32[]{:S(2)}) collective-permute-start(bf16[64,16,128]{2,1,0:T(8,128)(2,1)S(1)} %get-tuple-element.21), channel_id=1, source_target_pairs={{0,128},{128,0},{64,192},{192,64},{1,129},{129,1},{65,193},{193,65... | collective-permute-start | bytes 786440 | tf_op jit(solution)/shard_map/ppermute | solution.py:214
  50.0 6.4 %copy-start.1 = (bf16[1024,1024]{1,0:T(8,128)(2,1)S(1)}, bf16[1024,1024]{1,0:T(8,128)(2,1)}, u32[]{:S(2)}) copy-start(bf16[1024,1024]{1,0:T(8,128)(2,1)} %core_ref.3) | copy-start | bytes 6291460
  52.0 4.4 %collective-permute-start.5 = (bf16[1024,512]{1,0:T(8,128)(2,1)S(1)}, bf16[1024,512]{1,0:T(8,128)(2,1)S(1)}, u32[]{:S(2)}, u32[]{:S(2)}) collective-permute-start(bf16[1024,512]{1,0:T(8,128)(2,1)S(1)} %get-tuple-element.14.term0), channel_id=1, source_target_pairs={{0,64},{64,0},{128,192},{192,128},{1,65},{65,1},{129,193},{193,129... | collective-permute-start | bytes 3145736 | tf_op jit(solution)/shard_map/ppermute | solution.py:222
  55.6 2.9 %collective-permute-start.6 = (bf16[1024,512]{1,0:T(8,128)(2,1)S(1)}, bf16[1024,512]{1,0:T(8,128)(2,1)S(1)}, u32[]{:S(2)}, u32[]{:S(2)}) collective-permute-start(bf16[1024,512]{1,0:T(8,128)(2,1)S(1)} %get-tuple-element.16.term0), channel_id=1, source_target_pairs={{0,64},{64,0},{128,192},{192,128},{1,65},{65,1},{129,193},{193,129... | collective-permute-start | bytes 3145736 | tf_op jit(solution)/shard_map/ppermute | solution.py:224
  81.9 3.5 %collective-permute-start.7 = (bf16[64,8,256]{2,1,0:T(8,128)(2,1)S(1)}, bf16[64,8,256]{2,1,0:T(8,128)(2,1)S(1)}, u32[]{:S(2)}, u32[]{:S(2)}) collective-permute-start(bf16[64,8,256]{2,1,0:T(8,128)(2,1)S(1)} %all_to_all.11.rows_ref), channel_id=1, source_target_pairs={{0,64},{64,0},{128,192},{192,128},{1,65},{65,1},{129,193},{193,129... | collective-permute-start | bytes 786440 | tf_op jit(solution)/shard_map/ppermute | solution.py:238

commit v7 on v6

--- a/solution.py
+++ b/solution.py
@@ -63,7 +63,7 @@
     for kk in range(2):
         xq = points_of(x_ref, here, kk, pl.ds(half * HALF, HALF))
         v = dot(t_ref[kk], xq, NT)
-        own_ref[kk] = v
+        own_ref[kk] = v.astype(bf16)
         w = dot(t_ref[2 + kk], xq, NT)
         acc = v * v - w * w if acc is None else acc + (v * v - w * w)
     term_ref[...] = acc.astype(bf16)
@@ -104,7 +104,7 @@
         w = dot(jnp.concatenate([mix0[rows, :], mix1[rows, :]], axis=1), core_ref[...])
         for kk in range(2):
             own = jnp.concatenate([own0[kk, rows, :], own1[kk, rows, :]], axis=1)
-            source = (own * w).astype(bf16)
+            source = (own.astype(f32) * w).astype(bf16)
             tmp_ref[kk, rows, :] = dot(source, points_of(x_ref, here, kk, every)).astype(bf16)
     rows = [dot(points_of(x_ref, here, kk, every), tmp_ref[kk], TN).reshape(64, 4, NORB) for kk in range(2)]
     out_ref[...] = jnp.concatenate(rows, axis=1).astype(bf16)
@@ -179,7 +179,7 @@
 
 
 T_OUT = ((4, NPTS, NORB), bf16)
-OWN_OUT = ((2, NPTS, HALF), f32)
+OWN_OUT = ((2, NPTS, HALF), bf16)
 HALF_OUT = ((NPTS, HALF), bf16)
 
 

time: 86.6 us -> 86.7 us (level)
  no operation moved by 1% of the time
where the time goes in v7:
time: 86.7 us; the launch traced here: 86.5 us
  blocking collectives  49.9 us (58%)
  starting transfers between devices  14.3 us (16%)
  Pallas kernels  12.6 us (15%)
  waiting for transfers between devices  7.06 us (8%)
  local copies, waits for them, and re-layouts  1.9 us (2%)
    all_to_all x1, blocking collectives, local(): got = lax.all_to_all(msg, 'pa', 0, 0, tiled=True)  31.5 us
    all_to_all x1, blocking collectives, local(): back = lax.all_to_all(out, 'pa', 0, 0, tiled=True)  18.4 us
    ppermute x1, waiting for transfers between devices, local(): g_kind = to_green(lax.ppermute(got[:, :16], 'ta', CHIP_SWAP))  5.33 us
    ppermute x3, starting transfers between devices, local(): pieces.append(lax.ppermute(xpart, ('ta', 'pa'), square_pairs(s)))  5.16 us
    pallas_call x1, Pallas kernels, local(): call(fourth_kernel, 7, (((64, 8, NORB), bf16),), (HALF_OUT, HALF_OUT, ((2...  5 us
    ppermute x1, starting transfers between devices, local(): arrived = lax.ppermute(theirs, 'ta', CORE_SWAP)  3.29 us
    ppermute x1, starting transfers between devices, local(): back_next = lax.ppermute(back, 'ta', CORE_SWAP)  2.38 us
    ppermute x1, starting transfers between devices, local(): term0_next = lax.ppermute(term0, 'ta', CORE_SWAP)  2.13 us
  transfers between devices with their start and end apart: 8, of which 4 were waited for; matrix products, arithmetic and copies ran while one was open for 1% of the time, Pallas kernels for 5%

profile of v7, /device:TPU:1, one launch (start us, length us, event | category | flops | bytes accessed | tf_op | source)
XLA Modules:
  0.0 86.5 jit_solution(15813174832251084473)
XLA Ops:
  0.0 1.2 %dynamic-slice_bitcast_fusion = (bf16[64,1,2,4,256]{4,3,2,0,1:T(4,128)(2,1)S(1)}, bf16[64,1,2,4,256]{4,3,2,0,1:T(4,128)(2,1)S(1)}) fusion(bf16[64,2,2,4,256]{4,3,2,1,0:T(4,128)(2,1)} %bitcast.28, s32[]{:T(128)S(6)} %select_n.42, s32[]{:T(128)S(6)} %select_n.41), kind=kLoop, calls=%fused_computation.5 | loop fusion | bytes 1048584
  1.2 0.1 reshape.42
  1.3 3.3 %collective-permute-start = (bf16[64,8,256]{2,1,0:T(8,128)(2,1)S(1)}, bf16[64,8,256]{2,1,0:T(8,128)(2,1)S(1)}, u32[]{:S(2)}, u32[]{:S(2)}) collective-permute-start(bf16[64,8,256]{2,1,0:T(8,128)(2,1)S(1)} %reshape.42), channel_id=1, source_target_pairs={{0,64},{64,0},{128,192},{192,128},{1,65},{65,1},{129,193},{193,129... | collective-permute-start | bytes 786440 | tf_op jit(solution)/shard_map/ppermute | solution.py:202
  4.7 0.2 multiply_select_fusion
  4.9 0.1 broadcast_multiply_fusion
  5.0 0.1 reshape.41.rows_ref
  5.0 0.8 shard_map.38
  5.9 0.3 shard_map.39
  6.2 31.5 %all_to_all.10 = bf16[64,32,128]{2,1,0:T(8,128)(2,1)S(1)} all-to-all(bf16[64,32,128]{2,1,0:T(8,128)(2,1)S(1)} %shard_map.39), channel_id=1, replica_groups=mesh['ta'=4,'pa'=64] {'pa'}, dimensions={0} | all-to-all | bytes 1048576 | tf_op jit(solution)/shard_map/all_to_all | solution.py:210
  37.7 1.2 %collective-permute-start.3 = (bf16[1024,128]{1,0:T(8,128)(2,1)S(1)}, bf16[1024,128]{1,0:T(8,128)(2,1)S(1)}, u32[]{:S(2)}, u32[]{:S(2)}) collective-permute-start(bf16[1024,128]{1,0:T(8,128)(2,1)S(1)} %bitcast.24), channel_id=1, source_target_pairs={{0,20},{1,21},{2,22},{3,23},{4,16},{5,17},{6,18},{7,19},{8,28},{9,... | collective-permute-start | bytes 786440 | tf_op jit(solution)/shard_map/ppermute | solution.py:217
  39.0 1.6 %collective-permute-start.2 = (bf16[1024,128]{1,0:T(8,128)(2,1)S(1)}, bf16[1024,128]{1,0:T(8,128)(2,1)S(1)}, u32[]{:S(2)}, u32[]{:S(2)}) collective-permute-start(bf16[1024,128]{1,0:T(8,128)(2,1)S(1)} %bitcast.25), channel_id=1, source_target_pairs={{0,16},{1,17},{2,18},{3,19},{4,20},{5,21},{6,22},{7,23},{8,24},{9,... | collective-permute-start | bytes 786440 | tf_op jit(solution)/shard_map/ppermute | solution.py:217
  40.6 2.3 %collective-permute-start.1 = (bf16[1024,128]{1,0:T(8,128)(2,1)S(1)}, bf16[1024,128]{1,0:T(8,128)(2,1)S(1)}, u32[]{:S(2)}, u32[]{:S(2)}) collective-permute-start(bf16[1024,128]{1,0:T(8,128)(2,1)S(1)} %bitcast.26), channel_id=1, source_target_pairs={{0,4},{1,5},{2,6},{3,7},{4,0},{5,1},{6,2},{7,3},{8,12},{9,13},{10,... | collective-permute-start | bytes 786440 | tf_op jit(solution)/shard_map/ppermute | solution.py:217
  42.9 1.0 %collective-permute-start.4 = (bf16[64,16,128]{2,1,0:T(8,128)(2,1)S(1)}, bf16[64,16,128]{2,1,0:T(8,128)(2,1)S(1)}, u32[]{:S(2)}, u32[]{:S(2)}) collective-permute-start(bf16[64,16,128]{2,1,0:T(8,128)(2,1)S(1)} %get-tuple-element.21), channel_id=1, source_target_pairs={{0,128},{128,0},{64,192},{192,64},{1,129},{129,1},{65,193},{193,65... | collective-permute-start | bytes 786440 | tf_op jit(solution)/shard_map/ppermute | solution.py:214
  44.0 0.1 reshape.44
  44.0 0.1 copy.13
  44.2 5.3 %collective-permute-done.4 = bf16[64,16,128]{2,1,0:T(8,128)(2,1)S(1)} collective-permute-done((bf16[64,16,128]{2,1,0:T(8,128)(2,1)S(1)}, bf16[64,16,128]{2,1,0:T(8,128)(2,1)S(1)}, u32[]{:S(2)}, u32[]{:S(2)}) %collective-permute-start.4) | collective-permute-done | bytes 262176 | tf_op jit(solution)/shard_map/ppermute | solution.py:214
  49.7 0.1 copy.12
  49.9 0.1 pad_maximum_fusion.x_ref
  50.0 1.9 %shard_map.40 = (bf16[4,1024,256]{2,1,0:T(8,128)(2,1)S(1)}, bf16[2,1024,512]{2,1,0:T(8,128)(2,1)S(1)}, bf16[1024,512]{1,0:T(8,128)(2,1)S(1)}) custom-call(bf16[4,1024,128]{2,1,0:T(8,128)(2,1)S(1)} %pad_maximum_fusion.x_ref, bf16[2,256,256]{2,1,0:T(8,128)(2,1)S(1)} %reshape.45.g_mine, bf16[2,256,256]{2,1,0:T(8,128)(2,1)S(1)} %reshape.47.g_else), custom_call_target="tpu_custom_call" | custom-call | flops 1600000000 | bytes 2097152 | tf_op jit(solution)/shard_map/pallas_call | solution.py:221
  52.0 2.1 %collective-permute-start.5 = (bf16[1024,512]{1,0:T(8,128)(2,1)S(1)}, bf16[1024,512]{1,0:T(8,128)(2,1)S(1)}, u32[]{:S(2)}, u32[]{:S(2)}) collective-permute-start(bf16[1024,512]{1,0:T(8,128)(2,1)S(1)} %get-tuple-element.14.term0), channel_id=1, source_target_pairs={{0,64},{64,0},{128,192},{192,128},{1,65},{65,1},{129,193},{193,129... | collective-permute-start | bytes 3145736 | tf_op jit(solution)/shard_map/ppermute | solution.py:222
  54.1 1.4 %shard_map.42 = (bf16[2,1024,512]{2,1,0:T(8,128)(2,1)S(1)}, bf16[1024,512]{1,0:T(8,128)(2,1)S(1)}) custom-call(bf16[4,1024,128]{2,1,0:T(8,128)(2,1)S(1)} %pad_maximum_fusion.x_ref, bf16[4,1024,256]{2,1,0:T(8,128)(2,1)S(1)} %get-tuple-element.15.t_ref), custom_call_target="tpu_custom_call" | custom-call | flops 1100000000 | bytes 2097152 | tf_op jit(solution)/shard_map/pallas_call | solution.py:223
  55.6 0.3 collective-permute-start.6
  55.9 0.5 collective-permute-done.5.term1
  56.4 1.3 %shard_map.41.mix0 = bf16[1024,512]{1,0:T(8,128)(2,1)S(1)} custom-call(bf16[1024,1024]{1,0:T(8,128)(2,1)S(1)} %copy-done.1, bf16[1024,512]{1,0:T(8,128)(2,1)S(1)} %get-tuple-element.14.term0, bf16[1024,512]{1,0:T(8,128)(2,1)S(1)} %collective-permute-done.5.term1), custom_call_target="tpu_custom_call" | custom-call | flops 1100000000 | bytes 2097152 | tf_op jit(solution)/shard_map/pallas_call | solution.py:225
  57.7 0.8 collective-permute-done.6.term1
  58.5 5.0 %shard_map.43 = bf16[64,8,256]{2,1,0:T(8,128)(2,1)S(1)} custom-call(bf16[1024,1024]{1,0:T(8,128)(2,1)S(1)} %copy-done.1, bf16[1024,512]{1,0:T(8,128)(2,1)S(1)} %shard_map.41.mix0, bf16[1024,512]{1,0:T(8,128)(2,1)S(1)} %get-tuple-element.16.term0, bf16[1024,512]{1,0:T(8,128)(2,1)S(1)} %collective-permute-done.6.term1, ...), custom_call_target="tpu_custom_call" | custom-call | flops 4600000000 | bytes 2097152 | tf_op jit(solution)/shard_map/pallas_call | solution.py:228
  63.5 18.4 %all_to_all.11.rows_ref = bf16[64,8,256]{2,1,0:T(8,128)(2,1)S(1)} all-to-all(bf16[64,8,256]{2,1,0:T(8,128)(2,1)S(1)} %shard_map.43), channel_id=1, replica_groups=mesh['ta'=4,'pa'=64] {'pa'}, dimensions={0} | all-to-all | bytes 524288 | tf_op jit(solution)/shard_map/all_to_all | solution.py:237
  81.9 2.4 %collective-permute-start.7 = (bf16[64,8,256]{2,1,0:T(8,128)(2,1)S(1)}, bf16[64,8,256]{2,1,0:T(8,128)(2,1)S(1)}, u32[]{:S(2)}, u32[]{:S(2)}) collective-permute-start(bf16[64,8,256]{2,1,0:T(8,128)(2,1)S(1)} %all_to_all.11.rows_ref), channel_id=1, source_target_pairs={{0,64},{64,0},{128,192},{192,128},{1,65},{65,1},{129,193},{193,129... | collective-permute-start | bytes 786440 | tf_op jit(solution)/shard_map/ppermute | solution.py:238
  84.3 0.5 shard_map.37.table_ref
  84.7 0.3 shard_map.44.own_ref
  85.0 0.4 collective-permute-done.7.rows_ref
  85.4 1.1 %shard_map.45 = bf16[64,4,4,256]{3,2,1,0:T(4,128)(2,1)} custom-call(bf16[512,512]{1,0:T(8,128)(2,1)S(1)} %shard_map.37.table_ref, bf16[64,8,256]{2,1,0:T(8,128)(2,1)S(1)} %collective-permute-done.7.rows_ref, bf16[64,2,4,256]{3,2,1,0:T(4,128)(2,1)S(1)} %shard_map.44.own_ref), custom_call_target="tpu_custom_call" | custom-call | flops 300000000 | bytes 2097152 | tf_op jit(solution)/shard_map/pallas_call | solution.py:240
  (21 shorter events, 0.4 us)
Async XLA Ops:
  0.0 4.6 %copy-start = (bf16[4,256,16]{1,2,0:T(8,128)(2,1)S(1)}, bf16[4,256,16]{1,2,0:T(8,128)(2,1)}, u32[]{:S(2)}) copy-start(bf16[4,256,16]{1,2,0:T(8,128)(2,1)} %param.4) | copy-start | bytes 98308
  1.3 4.6 %collective-permute-start = (bf16[64,8,256]{2,1,0:T(8,128)(2,1)S(1)}, bf16[64,8,256]{2,1,0:T(8,128)(2,1)S(1)}, u32[]{:S(2)}, u32[]{:S(2)}) collective-permute-start(bf16[64,8,256]{2,1,0:T(8,128)(2,1)S(1)} %reshape.42), channel_id=1, source_target_pairs={{0,64},{64,0},{128,192},{192,128},{1,65},{65,1},{129,193},{193,129... | collective-permute-start | bytes 786440 | tf_op jit(solution)/shard_map/ppermute | solution.py:202
  37.7 12.1 %collective-permute-start.3 = (bf16[1024,128]{1,0:T(8,128)(2,1)S(1)}, bf16[1024,128]{1,0:T(8,128)(2,1)S(1)}, u32[]{:S(2)}, u32[]{:S(2)}) collective-permute-start(bf16[1024,128]{1,0:T(8,128)(2,1)S(1)} %bitcast.24), channel_id=1, source_target_pairs={{0,20},{1,21},{2,22},{3,23},{4,16},{5,17},{6,18},{7,19},{8,28},{9,... | collective-permute-start | bytes 786440 | tf_op jit(solution)/shard_map/ppermute | solution.py:217
  39.0 10.9 %collective-permute-start.2 = (bf16[1024,128]{1,0:T(8,128)(2,1)S(1)}, bf16[1024,128]{1,0:T(8,128)(2,1)S(1)}, u32[]{:S(2)}, u32[]{:S(2)}) collective-permute-start(bf16[1024,128]{1,0:T(8,128)(2,1)S(1)} %bitcast.25), channel_id=1, source_target_pairs={{0,16},{1,17},{2,18},{3,19},{4,20},{5,21},{6,22},{7,23},{8,24},{9,... | collective-permute-start | bytes 786440 | tf_op jit(solution)/shard_map/ppermute | solution.py:217
  40.6 9.3 %collective-permute-start.1 = (bf16[1024,128]{1,0:T(8,128)(2,1)S(1)}, bf16[1024,128]{1,0:T(8,128)(2,1)S(1)}, u32[]{:S(2)}, u32[]{:S(2)}) collective-permute-start(bf16[1024,128]{1,0:T(8,128)(2,1)S(1)} %bitcast.26), channel_id=1, source_target_pairs={{0,4},{1,5},{2,6},{3,7},{4,0},{5,1},{6,2},{7,3},{8,12},{9,13},{10,... | collective-permute-start | bytes 786440 | tf_op jit(solution)/shard_map/ppermute | solution.py:217
  42.9 6.7 %collective-permute-start.4 = (bf16[64,16,128]{2,1,0:T(8,128)(2,1)S(1)}, bf16[64,16,128]{2,1,0:T(8,128)(2,1)S(1)}, u32[]{:S(2)}, u32[]{:S(2)}) collective-permute-start(bf16[64,16,128]{2,1,0:T(8,128)(2,1)S(1)} %get-tuple-element.21), channel_id=1, source_target_pairs={{0,128},{128,0},{64,192},{192,64},{1,129},{129,1},{65,193},{193,65... | collective-permute-start | bytes 786440 | tf_op jit(solution)/shard_map/ppermute | solution.py:214
  52.0 4.4 %copy-start.1 = (bf16[1024,1024]{1,0:T(8,128)(2,1)S(1)}, bf16[1024,1024]{1,0:T(8,128)(2,1)}, u32[]{:S(2)}) copy-start(bf16[1024,1024]{1,0:T(8,128)(2,1)} %core_ref.3) | copy-start | bytes 6291460
  52.0 4.4 %collective-permute-start.5 = (bf16[1024,512]{1,0:T(8,128)(2,1)S(1)}, bf16[1024,512]{1,0:T(8,128)(2,1)S(1)}, u32[]{:S(2)}, u32[]{:S(2)}) collective-permute-start(bf16[1024,512]{1,0:T(8,128)(2,1)S(1)} %get-tuple-element.14.term0), channel_id=1, source_target_pairs={{0,64},{64,0},{128,192},{192,128},{1,65},{65,1},{129,193},{193,129... | collective-permute-start | bytes 3145736 | tf_op jit(solution)/shard_map/ppermute | solution.py:222
  55.6 2.9 %collective-permute-start.6 = (bf16[1024,512]{1,0:T(8,128)(2,1)S(1)}, bf16[1024,512]{1,0:T(8,128)(2,1)S(1)}, u32[]{:S(2)}, u32[]{:S(2)}) collective-permute-start(bf16[1024,512]{1,0:T(8,128)(2,1)S(1)} %get-tuple-element.16.term0), channel_id=1, source_target_pairs={{0,64},{64,0},{128,192},{192,128},{1,65},{65,1},{129,193},{193,129... | collective-permute-start | bytes 3145736 | tf_op jit(solution)/shard_map/ppermute | solution.py:224
  81.9 3.5 %collective-permute-start.7 = (bf16[64,8,256]{2,1,0:T(8,128)(2,1)S(1)}, bf16[64,8,256]{2,1,0:T(8,128)(2,1)S(1)}, u32[]{:S(2)}, u32[]{:S(2)}) collective-permute-start(bf16[64,8,256]{2,1,0:T(8,128)(2,1)S(1)} %all_to_all.11.rows_ref), channel_id=1, source_target_pairs={{0,64},{64,0},{128,192},{192,128},{1,65},{65,1},{129,193},{193,129... | collective-permute-start | bytes 786440 | tf_op jit(solution)/shard_map/ppermute | solution.py:238
